TPU v7x, 32 devices: a whole 2x2x4 slice. The times are simulated.
32 devices in a mesh: rep: 2 (over y), gx: 4 (over z), gy: 4 (over x, core).
Axes of the slice: x: 2, y: 2, z: 4, core: 2. Of those that a mesh axis runs over, the one named last changes fastest.
Arguments:
- positions: float32 [3, 8, 4, 1024], P(None, ('rep', 'gx'), 'gy'), parts along dimension 1, may hold values from 0 to 256, as said below
- charges: float32 [8, 4, 1024], P(('rep', 'gx'), 'gy'), parts along dimension 0, may hold values from -2 to 2
- pair_lists: int32 [8, 4, 4, 4], P(('rep', 'gx'), 'gy'), parts along dimension 0, may hold values from 0 to 35, as said below
- slab_dest: int32 [8, 4, 8], P(('rep', 'gx'), 'gy'), parts along dimension 0, may hold values from 0 to 3, as said below
- atom_counts: int32 [8, 4], P(('rep', 'gx'), 'gy'), parts along dimension 0, may hold values from 512 to 1024, as said below
Outputs:
- short_forces: float32 [3, 8, 4, 1024], P(None, ('rep', 'gx'), 'gy'), parts along dimension 1
- long_forces: float32 [3, 8, 4, 1024], P(None, ('rep', 'gx'), 'gy'), parts along dimension 1
There are 2 independent parts, one for each index of `rep`. A program takes and returns all parts, laid end to end along the dimension named above; each array names one. Nothing has to cross between parts.
Inputs may be any that keep to these rules, and one draw needn't show every extreme that they name: `positions`: the first coordinate lies in [0, 64), the second in [0, 64), and the third in the slab of the atom's block, [s * 32, (s + 1) * 32). `pair_lists`: each list names 4 different clusters of the neighbourhood, the cluster's own, 16 + c for cluster c, first; the others are clusters whose blocks' slabs lie nearest to those of the cluster's own blocks. `slab_dest`: the blocks of a cell name slabs in non-decreasing order; at most 4 blocks of one cell name one slab, and in every cell some slab is named by exactly 4. `atom_counts`: some cell holds 1024 atoms in every draw.
All inputs are finite; a program needn't handle non-finite values.
Results may differ from a plain program's by a relative error of at most 0.0003.
Values sent between devices are 32-bit elements; how exact they have to be, the bound alone decides.
A program may use at most 128 MiB of HBM per device.

v0:
```python
import jax
import jax.numpy as jnp
from jax import lax
from jax.sharding import PartitionSpec as P

GRID_X = 256
GRID_Y = 256
GRID_Z = 128


spacing = 0.16
ewald_split = 3.47
cutoff = 0.9
soft_core = 0.09
root_factor = 1.1283791670955126


def with_halo(value, sides, width):
    for axis, dim in sides:
        count, length = (lax.axis_size(axis), value.shape[dim])
        up = [(i, (i + 1) % count) for i in range(count)]
        down = [(j, i) for i, j in up]
        last = lax.slice_in_dim(value, length - width, length, axis=dim)
        initial = lax.slice_in_dim(value, 0, width, axis=dim)
        before = lax.ppermute(last, axis, up)
        after = lax.ppermute(initial, axis, down)
        value = jnp.concatenate([before, value, after], axis=dim)
    return value


def from_behind(value, axis, steps):
    count = lax.axis_size(axis)
    pairs = [(source, (source + steps) % count) for source in range(count)]
    return lax.ppermute(value, axis, pairs)


def product(pattern, left_side, right_side):
    return jnp.einsum(
        pattern,
        left_side,
        right_side,
        precision=lax.Precision.HIGHEST,
        preferred_element_type=jnp.float32,
    )


def spline_weights(fraction):
    remain = 1.0 - fraction
    square = fraction * fraction
    cube_part = square * fraction
    values = jnp.stack(
        [
            remain * remain * remain / 6.0,
            (3.0 * cube_part - 6.0 * square + 4.0) / 6.0,
            (-3.0 * cube_part + 3.0 * square + 3.0 * fraction + 1.0) / 6.0,
            cube_part / 6.0,
        ]
    )
    slopes = jnp.stack(
        [
            -0.5 * remain * remain,
            0.5 * (3.0 * square - 4.0 * fraction),
            0.5 * (-3.0 * square + 2.0 * fraction + 1.0),
            0.5 * square,
        ]
    )
    return (values, slopes)


def split_cells(coordinate, offset, cell_count):
    inside = coordinate - offset
    lowest = jnp.clip(jnp.floor(inside).astype(jnp.int32), 0, cell_count - 1)
    return (lowest, inside - lowest.astype(inside.dtype))


def spline_table(lowest, values, table_size):
    points = jnp.arange(table_size, dtype=jnp.int32)[None, :]
    lookup = jnp.zeros((lowest.shape[0], table_size), jnp.float32)
    for spline_term in range(4):
        lookup = lookup + jnp.where(
            points == (lowest[:, None] + spline_term) % table_size,
            values[spline_term][:, None],
            0.0,
        )
    return lookup


def dft_tables(sample_at, freq_at, period):
    winding = sample_at[:, None] * freq_at[None, :] % period
    phases = winding.astype(jnp.float32) * (2.0 * jnp.pi / period)
    return (jnp.cos(phases), jnp.sin(phases))


def influence(index_x, index_y, index_z):

    def signed(index, period):
        return jnp.where(index <= period // 2, index, index - period).astype(jnp.float32) / (
            period * spacing
        )

    def modulus(index, period):
        return ((2.0 + jnp.cos(index.astype(jnp.float32) * (2.0 * jnp.pi / period))) / 3.0) ** 2

    wave = (
        signed(index_x, GRID_X) ** 2 + signed(index_y, GRID_Y) ** 2 + signed(index_z, GRID_Z) ** 2
    )
    safe_wave = jnp.where(wave > 0.0, wave, 1.0)
    volume = GRID_X * GRID_Y * GRID_Z * spacing**3
    green = jnp.exp(-((jnp.pi / ewald_split) ** 2) * safe_wave) / (jnp.pi * volume * safe_wave)
    green = green / (modulus(index_x, GRID_X) * modulus(index_y, GRID_Y) * modulus(index_z, GRID_Z))
    return jnp.where(wave > 0.0, green, 0.0)


def cluster_forces(own_atoms, beside_all, pair_list):

    def one_cluster(inputs):
        own_rows, chosen = inputs
        partner = beside_all[:, chosen]
        offsets = (own_rows[:3, None, :, None] - partner[:3, :, None, :]) * spacing
        dist_square = jnp.sum(offsets * offsets, axis=0)
        soft_square = dist_square + soft_core
        soft_dist = jnp.sqrt(soft_square)
        scaled = ewald_split * soft_dist
        strength = (
            jax.scipy.special.erfc(scaled) / soft_dist
            + ewald_split * root_factor * jnp.exp(-scaled * scaled)
        ) / soft_square
        cutoff_taper = jnp.where(
            dist_square < cutoff * cutoff, (1.0 - dist_square / (cutoff * cutoff)) ** 2, 0.0
        )
        weight = partner[3][:, None, :] * strength * cutoff_taper
        return own_rows[3] * jnp.sum(weight[None] * offsets, axis=(1, 3))

    return lax.map(one_cluster, (jnp.moveaxis(own_atoms, 1, 0), pair_list))


def local(positions, charges, pair_lists, slab_dest, atom_counts):
    count_x = lax.axis_size("gx")
    count_y = lax.axis_size("gy")
    place_x = lax.axis_index("gx")
    place_y = lax.axis_index("gy")
    atom_total = positions.shape[3]
    clusters = pair_lists.shape[2]
    cluster_size = atom_total // clusters
    blocks = slab_dest.shape[2]
    block_size = atom_total // blocks
    cells_x = GRID_X // count_x
    cells_y = GRID_Y // count_y
    cells_z = GRID_Z // count_y
    living = jnp.arange(atom_total, dtype=jnp.int32) < atom_counts[0, 0]
    charge = jnp.where(living, charges[0, 0], 0.0)
    packed = jnp.concatenate([positions, charge[None, None, None, :]], axis=0)
    nearby = with_halo(packed, (("gx", 1), ("gy", 2)), 1)
    steps_x = (jnp.arange(3, dtype=jnp.float32) - 1.0) * cells_x
    steps_y = (jnp.arange(3, dtype=jnp.float32) - 1.0) * cells_y
    zero_grid = jnp.zeros((3, 3), jnp.float32)
    cell_shift = jnp.stack(
        [steps_x[:, None] + zero_grid, steps_y[None, :] + zero_grid, zero_grid, zero_grid]
    )
    beside_all = (nearby + cell_shift[:, :, :, None]).reshape(4, 9 * clusters, cluster_size)
    pair_part = cluster_forces(
        packed.reshape(4, clusters, cluster_size), beside_all, pair_lists[0, 0]
    )
    short_forces = jnp.moveaxis(pair_part, 1, 0).reshape(3, 1, 1, atom_total)
    fields = packed[:, 0, 0, :]
    slab_of = slab_dest[0, 0]
    member = (slab_of[:, None] == jnp.arange(count_y, dtype=jnp.int32)[None, :]).astype(jnp.int32)
    earlier = jnp.sum((jnp.cumsum(member, axis=0) - member) * member, axis=1)
    capacity = 2 * blocks // count_y
    target = slab_of * capacity + earlier
    placing = (target[:, None] == jnp.arange(count_y * capacity, dtype=jnp.int32)[None, :]).astype(
        jnp.float32
    )
    outgoing = product("fbk,bs->fsk", fields.reshape(4, blocks, block_size), placing)
    arrived = lax.all_to_all(
        outgoing.reshape(4, count_y, capacity, block_size),
        "gy",
        split_axis=1,
        concat_axis=1,
        tiled=True,
    )
    mesh_atoms = arrived.reshape(4, count_y * capacity * block_size)
    source = jnp.arange(count_y * capacity * block_size, dtype=jnp.int32) // (capacity * block_size)
    lowest_x, fraction_x = split_cells(mesh_atoms[0], 0.0, cells_x)
    lowest_y, fraction_y = split_cells(mesh_atoms[1], 0.0, cells_y)
    lowest_z, fraction_z = split_cells(
        mesh_atoms[2], (place_y * cells_z).astype(jnp.float32), cells_z
    )
    values_x, slopes_x = spline_weights(fraction_x)
    values_y, slopes_y = spline_weights(fraction_y)
    values_z, slopes_z = spline_weights(fraction_z)
    extent_x = cells_x + 3
    extent_z = cells_z + 3
    weight_x = spline_table(lowest_x, values_x, extent_x)
    slope_x = spline_table(lowest_x, slopes_x, extent_x)
    weight_z = spline_table(lowest_z, values_z, extent_z)
    slope_z = spline_table(lowest_z, slopes_z, extent_z)
    row_y = source * cells_y + lowest_y
    weight_y = spline_table(row_y, values_y, GRID_Y)
    slope_y = spline_table(row_y, slopes_y, GRID_Y)
    planes = (mesh_atoms[3][:, None, None] * weight_x[:, :, None] * weight_z[:, None, :]).reshape(
        -1, extent_x * extent_z
    )
    spread = product("ra,ry->ay", planes, weight_y).reshape(extent_x, extent_z, GRID_Y)
    carried_x = from_behind(spread[cells_x:], "gx", 1)
    charge_mesh = spread[:cells_x].at[:3].add(carried_x)
    carried_z = from_behind(charge_mesh[:, cells_z:], "gy", 1)
    charge_mesh = charge_mesh[:, :cells_z].at[:, :3].add(carried_z)
    index_x = jnp.arange(GRID_X, dtype=jnp.int32)
    index_y = jnp.arange(GRID_Y, dtype=jnp.int32)
    index_z = jnp.arange(GRID_Z, dtype=jnp.int32)
    cosine_x, sine_x = dft_tables(index_x, index_x, GRID_X)
    cosine_y, sine_y = dft_tables(index_y, index_y, GRID_Y)
    cosine_z, sine_z = dft_tables(index_z, index_z, GRID_Z)
    real_part = product("xzy,yk->xzk", charge_mesh, cosine_y)
    imag_part = -product("xzy,yk->xzk", charge_mesh, sine_y)
    rows_y = GRID_Y // count_x
    real_part, imag_part = (
        lax.all_to_all(
            lax.all_to_all(real_part, "gx", split_axis=2, concat_axis=0, tiled=True),
            "gy",
            split_axis=2,
            concat_axis=1,
            tiled=True,
        ),
        lax.all_to_all(
            lax.all_to_all(imag_part, "gx", split_axis=2, concat_axis=0, tiled=True),
            "gy",
            split_axis=2,
            concat_axis=1,
            tiled=True,
        ),
    )
    step_real = product("xzy,xk->kzy", real_part, cosine_x) + product(
        "xzy,xk->kzy", imag_part, sine_x
    )
    step_imag = product("xzy,xk->kzy", imag_part, cosine_x) - product(
        "xzy,xk->kzy", real_part, sine_x
    )
    wave_real = product("kzy,zl->kly", step_real, cosine_z) + product(
        "kzy,zl->kly", step_imag, sine_z
    )
    wave_imag = product("kzy,zl->kly", step_imag, cosine_z) - product(
        "kzy,zl->kly", step_real, sine_z
    )
    rows_t = rows_y // count_y
    green = influence(
        index_x[:, None, None],
        (place_x * rows_y + place_y * rows_t + jnp.arange(rows_t, dtype=jnp.int32))[None, None, :],
        index_z[None, :, None],
    )
    wave_real = wave_real * green
    wave_imag = wave_imag * green
    step_real = product("kly,zl->kzy", wave_real, cosine_z) - product(
        "kly,zl->kzy", wave_imag, sine_z
    )
    step_imag = product("kly,zl->kzy", wave_imag, cosine_z) + product(
        "kly,zl->kzy", wave_real, sine_z
    )
    plain_real = product("kzy,xk->xzy", step_real, cosine_x) - product(
        "kzy,xk->xzy", step_imag, sine_x
    )
    plain_imag = product("kzy,xk->xzy", step_imag, cosine_x) + product(
        "kzy,xk->xzy", step_real, sine_x
    )
    plain_real, plain_imag = (
        lax.all_to_all(
            lax.all_to_all(plain_real, "gx", split_axis=0, concat_axis=2, tiled=True),
            "gy",
            split_axis=1,
            concat_axis=2,
            tiled=True,
        ),
        lax.all_to_all(
            lax.all_to_all(plain_imag, "gx", split_axis=0, concat_axis=2, tiled=True),
            "gy",
            split_axis=1,
            concat_axis=2,
            tiled=True,
        ),
    )
    ordering = jnp.arange(GRID_Y, dtype=jnp.int32)
    sender_y = ordering // (count_x * rows_t)
    sender_x = ordering // rows_t % count_x
    freq_order = sender_x * rows_y + sender_y * rows_t + ordering % rows_t
    cosine_back, sine_back = dft_tables(freq_order, index_y, GRID_Y)
    potential = product("xzk,ky->xzy", plain_real, cosine_back) - product(
        "xzk,ky->xzy", plain_imag, sine_back
    )
    upper_x = from_behind(potential[:3], "gx", -1)
    wider = jnp.concatenate([potential, upper_x], axis=0)
    upper_z = from_behind(wider[:, :3], "gy", -1)
    wider = jnp.concatenate([wider, upper_z], axis=1).reshape(extent_x * extent_z, GRID_Y)
    level = product("ry,ay->ra", weight_y, wider).reshape(-1, extent_x, extent_z)
    level_slope = product("ry,ay->ra", slope_y, wider).reshape(-1, extent_x, extent_z)
    flat_z = jnp.sum(level * weight_z[:, None, :], axis=2)
    tilt_z = jnp.sum(level * slope_z[:, None, :], axis=2)
    tilt_y = jnp.sum(level_slope * weight_z[:, None, :], axis=2)
    factor = -mesh_atoms[3] / spacing
    mesh_forces = jnp.stack(
        [
            factor * jnp.sum(slope_x * flat_z, axis=1),
            factor * jnp.sum(weight_x * tilt_y, axis=1),
            factor * jnp.sum(weight_x * tilt_z, axis=1),
        ]
    )
    returned = lax.all_to_all(
        mesh_forces.reshape(3, count_y, capacity, block_size),
        "gy",
        split_axis=1,
        concat_axis=1,
        tiled=True,
    )
    far_part = product(
        "fsk,bs->fbk", returned.reshape(3, count_y * capacity, block_size), placing
    ).reshape(3, atom_total)
    return (short_forces, far_part.reshape(3, 1, 1, atom_total))


def solution(mesh):
    return jax.shard_map(
        local,
        mesh=mesh,
        in_specs=(
            P(None, ("rep", "gx"), "gy", None),
            P(("rep", "gx"), "gy", None),
            P(("rep", "gx"), "gy", None, None),
            P(("rep", "gx"), "gy", None),
            P(("rep", "gx"), "gy"),
        ),
        out_specs=(P(None, ("rep", "gx"), "gy", None), P(None, ("rep", "gx"), "gy", None)),
        check_vma=False,
    )
```

profile of v0, /device:TPU:0, one launch (start us, length us, event | category | flops | bytes accessed | tf_op | source)
XLA Modules:
  0.0 613.5 jit_solution(12395238515357369224)
XLA Ops:
  15.8 9.6 %broadcast_multiply_fusion = f32[2048,67,35]{0,1,2:T(8,128)} fusion(f32[2048,35]{0,1:T(8,128)S(1)} %get-tuple-element.112, f32[2048,67]{0,1:T(8,128)S(1)} %fusion.78), kind=kLoop, calls=%fused_computation.38 | loop fusion | flops 4802560 | bytes 20045824 | tf_op jit(solution)/shard_map/mul | solution.py:201
  25.5 22.1 %copy.218 = f32[2048,67,35]{0,2,1:T(8,128)} copy(f32[2048,67,35]{0,1,2:T(8,128)} %broadcast_multiply_fusion) | data formatting | bytes 38420480 | tf_op jit(solution)/shard_map/mul | solution.py:201
  47.5 16.6 %mul.989 = f32[2048,2345]{0,1:T(8,128)} reshape(f32[2048,67,35]{0,2,1:T(8,128)} %copy.218) | data formatting | bytes 38420480 | tf_op jit(solution)/shard_map/mul | solution.py:201
  64.1 20.7 %fusion.44 = f32[2345,256]{1,0:T(8,128)S(1)} fusion(f32[2048,2345]{0,1:T(8,128)} %mul.989, f32[2048]{0:T(1024)S(1)} %get-tuple-element.135, s32[2048]{0:T(1024)S(1)} %get-tuple-element.142, f32[2048]{0:T(1024)S(1)} %get-tuple-element.136, s32[2048]{0:T(1024)S(1)} %get-tuple-element.143, f32[2048]{0:T(1024)S(1)} %get-tuple-element.134, ...), kind=kOutput, calls=%fused_computation.77 | convolution fusion | flops 14759231488 | bytes 21677056 | tf_op jit(solution)/shard_map/ra,ry->ay/dot_general | solution.py:38
  108.5 5.6 copy.219
  114.0 5.5 reshape.1451
  128.2 5.6 copy.226
  139.3 31.2 %all-to-all-done.1 = f32[4,1,131072]{2,1,0:T(1,128)} async-done(((f32[4,1,131072]{2,1,0:T(1,128)}), f32[4,1,131072]{2,1,0:T(1,128)}, u32[]{:S(2)}, u32[]{:S(2)}) %all-to-all-start.1) | async-done | bytes 2097184 | tf_op jit(solution)/shard_map/all_to_all | solution.py:220
  175.7 7.7 %reduce.10 = f32[4,131072]{1,0:T(4,128)S(1)} reduce(f32[4,1,131072]{2,1,0:T(1,128)} %all-to-all-done.1, f32[]{:T(128)} %broadcast.2348), dimensions={1}, to_apply=%all_to_all.111.reduce_sub_computation | reduce | bytes 4194308 | tf_op jit(solution)/shard_map/all_to_all | solution.py:220
  187.4 6.9 %copy.308 = f32[64,32,4,64]{0,2,3,1:T(4,128)} copy(f32[64,32,4,64]{0,1,3,2:T(8,128)} %bitcast.217) | data formatting | bytes 4194304 | tf_op jit(solution)/shard_map/all_to_all | solution.py:220
  201.3 21.6 %all-to-all-done.3 = f32[4,1,131072]{2,1,0:T(1,128)} async-done(((f32[4,1,131072]{2,1,0:T(1,128)}), f32[4,1,131072]{2,1,0:T(1,128)}, u32[]{:S(2)}, u32[]{:S(2)}) %all-to-all-start.3) | async-done | bytes 2097184 | tf_op jit(solution)/shard_map/all_to_all | solution.py:227
  227.5 7.7 %reduce.9 = f32[4,131072]{1,0:T(4,128)S(1)} reduce(f32[4,1,131072]{2,1,0:T(1,128)} %all-to-all-done.3, f32[]{:T(128)} %broadcast.2348), dimensions={1}, to_apply=%all_to_all.119.reduce_sub_computation | reduce | bytes 4194308 | tf_op jit(solution)/shard_map/all_to_all | solution.py:227
  239.1 6.9 %copy.307 = f32[64,32,4,64]{0,2,3,1:T(4,128)} copy(f32[64,32,4,64]{0,1,3,2:T(8,128)} %bitcast.219) | data formatting | bytes 4194304 | tf_op jit(solution)/shard_map/all_to_all | solution.py:227
  268.3 15.1 %all-to-all-done.4 = f32[256,32,64]{0,1,2:T(8,128)} async-done(((f32[256,32,64]{0,1,2:T(8,128)}), f32[256,32,64]{0,1,2:T(8,128)}, u32[]{:S(2)}, u32[]{:S(2)}) %all-to-all-start.4) | async-done | bytes 2097184 | tf_op jit(solution)/shard_map/all_to_all | solution.py:226
  344.7 38.2 %all-to-all-done.7 = f32[256,128,16]{1,2,0:T(8,128)} async-done(((f32[256,128,16]{1,2,0:T(8,128)}), f32[256,128,16]{1,2,0:T(8,128)}, u32[]{:S(2)}, u32[]{:S(2)}) %all-to-all-start.7) | async-done | bytes 2097184 | tf_op jit(solution)/shard_map/all_to_all | solution.py:275
  399.5 35.8 %all-to-all-done.5 = f32[256,128,16]{1,2,0:T(8,128)} async-done(((f32[256,128,16]{1,2,0:T(8,128)}), f32[256,128,16]{1,2,0:T(8,128)}, u32[]{:S(2)}, u32[]{:S(2)}) %all-to-all-start.5) | async-done | bytes 2097184 | tf_op jit(solution)/shard_map/all_to_all | solution.py:268
  451.7 13.8 %all-to-all-done.8 = f32[4,1,131072]{2,1,0:T(1,128)} async-done(((f32[4,1,131072]{2,1,0:T(1,128)}), f32[4,1,131072]{2,1,0:T(1,128)}, u32[]{:S(2)}, u32[]{:S(2)}) %all-to-all-start.8) | async-done | bytes 2097184 | tf_op jit(solution)/shard_map/all_to_all | solution.py:274
  475.7 7.7 %reduce.12 = f32[4,131072]{1,0:T(4,128)S(1)} reduce(f32[4,1,131072]{2,1,0:T(1,128)} %all-to-all-done.8, f32[]{:T(128)} %broadcast.2348), dimensions={1}, to_apply=%all_to_all.139.reduce_sub_computation | reduce | bytes 4194308 | tf_op jit(solution)/shard_map/all_to_all | solution.py:274
  487.4 6.8 %copy.258 = f32[64,32,4,64]{3,2,1,0:T(4,128)} copy(f32[64,32,4,64]{3,0,1,2:T(8,128)} %bitcast.221) | data formatting | bytes 4194304 | tf_op jit(solution)/shard_map/all_to_all | solution.py:274
  499.7 7.7 %reduce.11 = f32[4,131072]{1,0:T(4,128)S(1)} reduce(f32[4,1,131072]{2,1,0:T(1,128)} %all-to-all-done.6, f32[]{:T(128)} %broadcast.2348), dimensions={1}, to_apply=%all_to_all.131.reduce_sub_computation | reduce | bytes 4194308 | tf_op jit(solution)/shard_map/all_to_all | solution.py:267
  511.4 6.9 %copy.251 = f32[64,32,4,64]{3,2,1,0:T(4,128)} copy(f32[64,32,4,64]{3,0,1,2:T(8,128)} %bitcast.222) | data formatting | bytes 4194304 | tf_op jit(solution)/shard_map/all_to_all | solution.py:267
  539.8 23.6 %multiply_reduce_fusion.2 = (f32[2048,67]{0,1:T(8,128)S(1)}, f32[2048,67]{0,1:T(8,128)S(1)}) fusion(f32[2048,35]{0,1:T(8,128)S(1)} %get-tuple-element.112, f32[2048,35]{0,1:T(8,128)S(1)} %get-tuple-element.111, f32[67,35,256]{2,1,0:T(8,128)S(1)} %pad_maximum_fusion, f32[2048]{0:T(1024)S(1)} %copy-done.25, s32[2048]{0:T(1024)S(1)} %get-tuple-element.142, ...), kind=kOutput, calls=%fused_computation.37 | convolution fusion | flops 14778167296 | bytes 4137984 | tf_op jit(solution)/shard_map/ry,ay->ra/dot_general | solution.py:38
  563.5 21.0 %multiply_reduce_fusion.1 = f32[2048,67]{0,1:T(8,128)S(1)} fusion(f32[2048,35]{0,1:T(8,128)S(1)} %get-tuple-element.112, f32[67,35,256]{2,1,0:T(8,128)S(1)} %pad_maximum_fusion, f32[2048]{0:T(1024)S(1)} %copy-done.36, f32[2048]{0:T(1024)S(1)} %copy-done.37, f32[2048]{0:T(1024)S(1)} %copy-done.35, f32[2048]{0:T(1024)S(1)} %copy-done.34, ...), kind=kOutput, calls=%fused_computation.36 | convolution fusion | flops 14768699392 | bytes 3302400 | tf_op jit(solution)/shard_map/ry,ay->ra/dot_general | solution.py:38
  589.8 21.7 %while.12 = (s32[]{:T(128)}, f32[4,3,256]{2,1,0:T(4,128)S(1)}, f32[4,4,256]{2,0,1:T(4,128)S(1)}, s32[4,4]{1,0:T(4,128)}, f32[4,36,256]{2,0,1:T(4,128)S(1)}, /*index=5*/s32[]{:T(128)}, s32[]{:T(128)}, s32[]{}) while((s32[]{:T(128)}, f32[4,3,256]{2,1,0:T(4,128)S(1)}, f32[4,4,256]{2,0,1:T(4,128)S(1)}, s32[4,4]{1,0:T(4,128)}, ...), condition=%wide.region_3.4_spmd, body=%wide.region_0.3_spmd.sunk | while | flops 25166860 | bytes 4333749 | solution.py:134
  (269 shorter events, 266.1 us)
Async XLA Ops:
  5.7 8.2 %all-to-all-start = ((f32[4,4,4,128]{3,2,0,1:T(4,128)}), f32[4,4,4,128]{3,2,0,1:T(4,128)S(1)}, u32[]{:S(2)}, u32[]{:S(2)}) async-start(f32[4,4,4,128]{3,2,0,1:T(4,128)} %copy.217), calls=%async_computation | async-start | bytes 65536 | tf_op jit(solution)/shard_map/all_to_all | solution.py:175
  15.4 48.7 %copy-start.24 = (f32[2048]{0:T(1024)}, f32[2048]{0:T(1024)S(1)}, u32[]{:S(2)}) copy-start(f32[2048]{0:T(1024)S(1)} %get-tuple-element.135) | copy-start | bytes 24580
  15.4 48.7 %copy-start.26 = (f32[2048]{0:T(1024)}, f32[2048]{0:T(1024)S(1)}, u32[]{:S(2)}) copy-start(f32[2048]{0:T(1024)S(1)} %get-tuple-element.136) | copy-start | bytes 24580
  15.4 48.7 %copy-start.28 = (f32[2048]{0:T(1024)}, f32[2048]{0:T(1024)S(1)}, u32[]{:S(2)}) copy-start(f32[2048]{0:T(1024)S(1)} %get-tuple-element.138) | copy-start | bytes 24580
  85.5 7.6 %collective-permute-start.4 = (f32[3,35,256]{2,1,0:T(8,128)}, f32[3,35,256]{2,1,0:T(8,128)}, u32[]{:S(2)}, u32[]{:S(2)}) collective-permute-start(f32[3,35,256]{2,1,0:T(8,128)} %slice.114), channel_id=1, source_target_pairs={{0,4},{4,8},{8,12},{12,0},{1,5},{5,9},{9,13},{13,1},{2,6},{6,10},{... | collective-permute-start | bytes 322568 | tf_op jit(solution)/shard_map/ppermute | solution.py:34
  95.5 5.9 collective-permute-start.5
  119.6 50.9 %all-to-all-start.1 = ((f32[4,1,131072]{2,1,0:T(1,128)}), f32[4,1,131072]{2,1,0:T(1,128)}, u32[]{:S(2)}, u32[]{:S(2)}) async-start(f32[4,1,131072]{2,1,0:T(1,128)} %reshape.1451), calls=%async_computation.1 | async-start | bytes 4194304 | tf_op jit(solution)/shard_map/all_to_all | solution.py:220
  170.5 52.5 %all-to-all-start.3 = ((f32[4,1,131072]{2,1,0:T(1,128)}), f32[4,1,131072]{2,1,0:T(1,128)}, u32[]{:S(2)}, u32[]{:S(2)}) async-start(f32[4,1,131072]{2,1,0:T(1,128)} %reshape.1449), calls=%async_computation.3 | async-start | bytes 4194304 | tf_op jit(solution)/shard_map/all_to_all | solution.py:227
  223.0 30.2 %all-to-all-start.2 = ((f32[256,32,64]{0,1,2:T(8,128)}), f32[256,32,64]{0,1,2:T(8,128)}, u32[]{:S(2)}, u32[]{:S(2)}) async-start(f32[256,32,64]{0,1,2:T(8,128)} %copy.221), calls=%async_computation.2 | async-start | bytes 4194304 | tf_op jit(solution)/shard_map/all_to_all | solution.py:219
  253.2 30.2 %all-to-all-start.4 = ((f32[256,32,64]{0,1,2:T(8,128)}), f32[256,32,64]{0,1,2:T(8,128)}, u32[]{:S(2)}, u32[]{:S(2)}) async-start(f32[256,32,64]{0,1,2:T(8,128)} %copy.228), calls=%async_computation.4 | async-start | bytes 4194304 | tf_op jit(solution)/shard_map/all_to_all | solution.py:226
  330.0 52.9 %all-to-all-start.7 = ((f32[256,128,16]{1,2,0:T(8,128)}), f32[256,128,16]{1,2,0:T(8,128)}, u32[]{:S(2)}, u32[]{:S(2)}) async-start(f32[256,128,16]{1,2,0:T(8,128)} %copy.254), calls=%async_computation.7 | async-start | bytes 4194304 | tf_op jit(solution)/shard_map/all_to_all | solution.py:275
  383.0 52.3 %all-to-all-start.5 = ((f32[256,128,16]{1,2,0:T(8,128)}), f32[256,128,16]{1,2,0:T(8,128)}, u32[]{:S(2)}, u32[]{:S(2)}) async-start(f32[256,128,16]{1,2,0:T(8,128)} %copy.247), calls=%async_computation.5 | async-start | bytes 4194304 | tf_op jit(solution)/shard_map/all_to_all | solution.py:268
  435.3 30.2 %all-to-all-start.8 = ((f32[4,1,131072]{2,1,0:T(1,128)}), f32[4,1,131072]{2,1,0:T(1,128)}, u32[]{:S(2)}, u32[]{:S(2)}) async-start(f32[4,1,131072]{2,1,0:T(1,128)} %reshape.1455), calls=%async_computation.8 | async-start | bytes 4194304 | tf_op jit(solution)/shard_map/all_to_all | solution.py:274
  465.5 34.2 %all-to-all-start.6 = ((f32[4,1,131072]{2,1,0:T(1,128)}), f32[4,1,131072]{2,1,0:T(1,128)}, u32[]{:S(2)}, u32[]{:S(2)}) async-start(f32[4,1,131072]{2,1,0:T(1,128)} %reshape.1453), calls=%async_computation.6 | async-start | bytes 4194304 | tf_op jit(solution)/shard_map/all_to_all | solution.py:267
  470.0 58.5 %collective-permute-start = (f32[4,1,1,1024]{3,2,1,0:T(1,128)S(1)}, f32[4,1,1,1024]{3,2,1,0:T(1,128)S(1)}, u32[]{:S(2)}, u32[]{:S(2)}) collective-permute-start(f32[4,1,1,1024]{3,2,1,0:T(1,128)S(1)} %pad_maximum_fusion.4), channel_id=1, source_target_pairs={{0,4},{4,8},{8,12},{12,0},{1,5},{5,9},{9,13},{13,1},{2,6},{6,10},{... | collective-permute-start | bytes 49160 | tf_op jit(solution)/shard_map/ppermute | solution.py:25
  470.1 58.4 %collective-permute-start.1 = (f32[4,1,1,1024]{3,2,1,0:T(1,128)S(1)}, f32[4,1,1,1024]{3,2,1,0:T(1,128)S(1)}, u32[]{:S(2)}, u32[]{:S(2)}) collective-permute-start(f32[4,1,1,1024]{3,2,1,0:T(1,128)S(1)} %pad_maximum_fusion.4), channel_id=1, source_target_pairs={{4,0},{8,4},{12,8},{0,12},{5,1},{9,5},{13,9},{1,13},{6,2},{10,6},{... | collective-permute-start | bytes 49160 | tf_op jit(solution)/shard_map/ppermute | solution.py:26
  528.5 4.7 collective-permute-start.6
  528.6 5.5 collective-permute-start.2
  528.7 5.5 collective-permute-start.3
  533.9 4.6 collective-permute-start.7
  539.7 23.6 %copy-start.34 = (f32[2048]{0:T(1024)S(1)}, f32[2048]{0:T(1024)}, u32[]{:S(2)}) copy-start(f32[2048]{0:T(1024)} %get-tuple-element.133) | copy-start | bytes 24580
  539.8 23.6 %copy-start.35 = (f32[2048]{0:T(1024)S(1)}, f32[2048]{0:T(1024)}, u32[]{:S(2)}) copy-start(f32[2048]{0:T(1024)} %get-tuple-element.137) | copy-start | bytes 24580
  539.8 23.6 %copy-start.36 = (f32[2048]{0:T(1024)S(1)}, f32[2048]{0:T(1024)}, u32[]{:S(2)}) copy-start(f32[2048]{0:T(1024)} %get-tuple-element.139) | copy-start | bytes 24580
  586.5 25.6 %all-to-all-start.9 = ((f32[3,4,4,128]{3,2,0,1:T(4,128)}), f32[3,4,4,128]{3,2,0,1:T(4,128)S(1)}, u32[]{:S(2)}, u32[]{:S(2)}) async-start(f32[3,4,4,128]{3,2,0,1:T(4,128)} %pad_maximum_fusion.3), calls=%async_computation.9 | async-start | bytes 49152 | tf_op jit(solution)/shard_map/all_to_all | solution.py:307
  (34 other events, 468.1 us)
where the time goes:
time: 625 us; the launch traced here: 613 us
  local copies, waits for them, and re-layouts  185 us (30%)
  waiting for transfers between devices  173 us (28%)
  matrix products  129 us (21%)
  other arithmetic  71.1 us (11%)
  starting transfers between devices  52.2 us (8%)
    dot_general x25, matrix products, product(): jnp.einsum(pattern, left_side, right_side, precision=lax.Precision.HIGHES...  129 us
    unnamed x89, local copies, waits for them, and re-layouts  40.1 us
    mul x2, local copies, waits for them, and re-layouts, local(): mesh_atoms[3][:, None, None] * weight_x[:, :, None] * weight_z[:, None, :]  38.6 us
    all_to_all x1, waiting for transfers between devices, local(): lax.all_to_all(plain_imag, 'gx', split_axis=0, concat_axis=2, tiled=True)  38.2 us
    all_to_all x1, waiting for transfers between devices, local(): lax.all_to_all(plain_real, 'gx', split_axis=0, concat_axis=2, tiled=True)  35.8 us
    all_to_all x1, waiting for transfers between devices, local(): lax.all_to_all(real_part, 'gx', split_axis=2, concat_axis=0, tiled=True)  31.2 us
    all_to_all x1, waiting for transfers between devices, local(): lax.all_to_all(imag_part, 'gx', split_axis=2, concat_axis=0, tiled=True)  21.6 us
    all_to_all x1, waiting for transfers between devices, local(): lax.all_to_all(lax.all_to_all(imag_part, 'gx', split_axis=2, concat_axis=...  15.1 us
  transfers between devices with their start and end apart: 18, of which 12 were waited for; matrix products, arithmetic and copies ran while one was open for 29% of the time, Pallas kernels for 0%

commit v1 on v0

v1 whole, which is shorter than its diff:
```python
import functools
import math

import jax
import jax.numpy as jnp
import numpy as np
from jax import lax
from jax.experimental import pallas as pl
from jax.experimental.pallas import tpu as pltpu
from jax.sharding import PartitionSpec as P

GRID_X = 256
GRID_Y = 256
GRID_Z = 128


spacing = 0.16
ewald_split = 3.47
cutoff = 0.9
soft_core = 0.09
root_factor = 1.1283791670955126
rows_group = 8


def with_halo(value, sides, width):
    for axis, dim in sides:
        count, length = (lax.axis_size(axis), value.shape[dim])
        up = [(i, (i + 1) % count) for i in range(count)]
        down = [(j, i) for i, j in up]
        last = lax.slice_in_dim(value, length - width, length, axis=dim)
        initial = lax.slice_in_dim(value, 0, width, axis=dim)
        before = lax.ppermute(last, axis, up)
        after = lax.ppermute(initial, axis, down)
        value = jnp.concatenate([before, value, after], axis=dim)
    return value


def moved(value, step_x, step_y):
    count_x = lax.axis_size("gx")
    count_y = lax.axis_size("gy")
    pairs = [
        (i * count_y + j, (i + step_x) % count_x * count_y + (j + step_y) % count_y)
        for i in range(count_x)
        for j in range(count_y)
    ]
    return lax.ppermute(value, ("gx", "gy"), pairs)


def round_up(value, multiple):
    return -(-value // multiple) * multiple


def hartley(period):
    turns = np.outer(np.arange(period), np.arange(period)) % period
    phases = turns * (2.0 * np.pi / period)
    return (np.cos(phases) + np.sin(phases)).astype(np.float32)


def halves(value):
    high = value.astype(jnp.bfloat16)
    low = (value - high.astype(jnp.float32)).astype(jnp.bfloat16)
    return (high, low)


def dot(left_side, right_side):
    return jnp.dot(left_side, right_side, preferred_element_type=jnp.float32)


def spline_weights(fraction):
    remain = 1.0 - fraction
    square = fraction * fraction
    cube_part = square * fraction
    values = [
        remain * remain * remain / 6.0,
        (3.0 * cube_part - 6.0 * square + 4.0) / 6.0,
        (-3.0 * cube_part + 3.0 * square + 3.0 * fraction + 1.0) / 6.0,
        cube_part / 6.0,
    ]
    slopes = [
        -0.5 * remain * remain,
        0.5 * (3.0 * square - 4.0 * fraction),
        0.5 * (-3.0 * square + 2.0 * fraction + 1.0),
        0.5 * square,
    ]
    return (values, slopes)


def split_cells(coordinate, offset, cell_count):
    inside = coordinate - offset
    lowest = jnp.clip(jnp.floor(inside).astype(jnp.int32), 0, cell_count - 1)
    return (lowest, inside - lowest.astype(inside.dtype))


def spline_table(lowest, values, table_size, period=None):
    points = lax.broadcasted_iota(jnp.int32, (table_size, lowest.shape[1]), 0)
    lookup = jnp.zeros(points.shape, jnp.float32)
    for spline_term in range(4):
        at = lowest + spline_term
        if period is not None:
            at = jnp.where(at >= period, at - period, at)
        lookup = jnp.where(points == at, values[spline_term], lookup)
    return lookup


def spread_kernel(cells, pad, atoms_ref, base_ref, turn_ref, out_ref, wx_ref, wy_ref, wz_ref, hi_ref, lo_ref):
    cells_x, cells_y, cells_z = cells
    pad_x, pad_y = pad
    atom_total = atoms_ref.shape[1]
    low_x, frac_x = split_cells(atoms_ref[0:1, :], 0.0, cells_x)
    low_y, frac_y = split_cells(atoms_ref[1:2, :], 0.0, cells_y)
    base = base_ref[...]
    low_z, frac_z = split_cells(atoms_ref[2:3, :], base.astype(jnp.float32), cells_z)
    wx_ref[...] = spline_table(low_x, spline_weights(frac_x)[0], pad_x) * atoms_ref[3:4, :]
    wy_ref[...] = spline_table(low_y, spline_weights(frac_y)[0], pad_y)
    turn = turn_ref[...]
    size_z = turn.shape[0]
    table_z = spline_table(base + low_z, spline_weights(frac_z)[0], size_z, size_z)
    waves = jnp.dot(
        turn, table_z, precision=lax.Precision.HIGHEST, preferred_element_type=jnp.float32
    ).T
    high, low = halves(waves)
    wz_ref[:, :size_z] = high
    wz_ref[:, size_z:] = low

    @pl.loop(0, pad_x // rows_group)
    def _(chunk):
        for inner in range(rows_group):
            row = wx_ref[pl.ds(chunk * rows_group + inner, 1), :]
            high, low = halves(row * wy_ref[...])
            hi_ref[pl.ds(inner * pad_y, pad_y), :] = high
            lo_ref[pl.ds(inner * pad_y, pad_y), :] = low
        both = dot(hi_ref[...], wz_ref[...])
        rest = dot(lo_ref[...], wz_ref[:, :size_z])
        total = both[:, :size_z] + both[:, size_z:] + rest
        out_ref[pl.ds(chunk * rows_group, rows_group)] = total.reshape(rows_group, pad_y, size_z)


def gather_kernel(cells, pad, atoms_ref, base_ref, turn_ref, mesh_ref, out_ref, wx_ref, vx_ref, wy_ref, vy_ref, wz_ref, level_ref):
    cells_x, cells_y, cells_z = cells
    pad_x, pad_y = pad
    atom_total = atoms_ref.shape[1]
    low_x, frac_x = split_cells(atoms_ref[0:1, :], 0.0, cells_x)
    low_y, frac_y = split_cells(atoms_ref[1:2, :], 0.0, cells_y)
    base = base_ref[...]
    low_z, frac_z = split_cells(atoms_ref[2:3, :], base.astype(jnp.float32), cells_z)
    values, slopes = spline_weights(frac_x)
    wx_ref[...] = spline_table(low_x, values, pad_x)
    vx_ref[...] = spline_table(low_x, slopes, pad_x)
    values, slopes = spline_weights(frac_y)
    wy_ref[...] = spline_table(low_y, values, pad_y)
    vy_ref[...] = spline_table(low_y, slopes, pad_y)
    values, slopes = spline_weights(frac_z)
    turn = turn_ref[...]
    size_z = turn.shape[0]
    for place, terms in enumerate((values, slopes)):
        table_z = spline_table(base + low_z, terms, size_z, size_z)
        waves = jnp.dot(
            turn, table_z, precision=lax.Precision.HIGHEST, preferred_element_type=jnp.float32
        )
        high, low = halves(waves)
        wz_ref[:size_z, pl.ds(place * atom_total, atom_total)] = high
        wz_ref[size_z:, pl.ds(place * atom_total, atom_total)] = low
    groups = pad_y // 8

    def one_chunk(chunk, sums):
        rows = mesh_ref[pl.ds(chunk * rows_group, rows_group)].reshape(rows_group * pad_y, size_z)
        high, low = halves(rows)
        level_ref[...] = dot(jnp.concatenate([high, high], axis=1), wz_ref[...]) + dot(
            low, wz_ref[:size_z, :]
        )
        first, second, third = sums
        for inner in range(rows_group):
            flat = level_ref[pl.ds(inner * pad_y, pad_y), :atom_total]
            tilt = level_ref[pl.ds(inner * pad_y, pad_y), atom_total:]
            across = wy_ref[...]
            part_x = jnp.sum((across * flat).reshape(groups, 8, atom_total), axis=0)
            part_y = jnp.sum((vy_ref[...] * flat).reshape(groups, 8, atom_total), axis=0)
            part_z = jnp.sum((across * tilt).reshape(groups, 8, atom_total), axis=0)
            weight = wx_ref[pl.ds(chunk * rows_group + inner, 1), :]
            slope = vx_ref[pl.ds(chunk * rows_group + inner, 1), :]
            first = first + slope * part_x
            second = second + weight * part_y
            third = third + weight * part_z
        return (first, second, third)

    zero = jnp.zeros((8, atom_total), jnp.float32)
    sums = lax.fori_loop(0, pad_x // rows_group, one_chunk, (zero, zero, zero))
    factor = -atoms_ref[3:4, :] / spacing
    for place in range(3):
        out_ref[pl.ds(place, 1), :] = factor * jnp.sum(sums[place], axis=0, keepdims=True)


def wave_kernel(mesh_ref, xh_ref, xl_ref, yh_ref, yl_ref, column_ref, row_ref, depth_ref, out_ref):
    def across(value):
        high, low = halves(value)
        return dot(xh_ref[...], high) + dot(xl_ref[...], high) + dot(xh_ref[...], low)

    def along(value):
        high, low = halves(value)
        return dot(high, yh_ref[...]) + dot(high, yl_ref[...]) + dot(low, yh_ref[...])

    waves = along(across(mesh_ref[0]))
    square = column_ref[:, 0:1] + row_ref[0:1, :] + depth_ref[0, 0:1, 0:1]
    scale = column_ref[:, 1:2] * row_ref[1:2, :] * depth_ref[0, 0:1, 1:2]
    green = jnp.where(square > 0.0, scale / jnp.where(square > 0.0, square, 1.0), 0.0)
    out_ref[0] = across(along(waves * green))


def green_factors(index, period):
    signed = jnp.where(index <= period // 2, index, index - period).astype(jnp.float32) / (
        period * spacing
    )
    modulus = ((2.0 + jnp.cos(index.astype(jnp.float32) * (2.0 * jnp.pi / period))) / 3.0) ** 2
    square = signed * signed
    return jnp.stack([square, jnp.exp(-((jnp.pi / ewald_split) ** 2) * square) / modulus])


def one_cluster(own_rows, partner):
    offsets = (own_rows[:3, :, None] - partner[:3, None, :]) * spacing
    dist_square = jnp.sum(offsets * offsets, axis=0)
    soft_square = dist_square + soft_core
    soft_dist = jnp.sqrt(soft_square)
    scaled = ewald_split * soft_dist
    strength = (
        jax.scipy.special.erfc(scaled) / soft_dist
        + ewald_split * root_factor * jnp.exp(-scaled * scaled)
    ) / soft_square
    cutoff_taper = jnp.where(
        dist_square < cutoff * cutoff, (1.0 - dist_square / (cutoff * cutoff)) ** 2, 0.0
    )
    weight = partner[3][None, :] * strength * cutoff_taper
    return own_rows[3] * jnp.sum(weight[None] * offsets, axis=2)


def convolved_by_planes(charge_mesh, count_x, count_y):
    cells_x, cells_y = charge_mesh.shape[:2]
    devices = count_x * count_y
    place = lax.axis_index("gx") * count_y + lax.axis_index("gy")
    depth = GRID_Z // devices
    outgoing = jnp.transpose(charge_mesh.reshape(cells_x * cells_y, GRID_Z)).reshape(
        devices, depth, cells_x * cells_y
    )
    arrived = lax.all_to_all(outgoing, ("gx", "gy"), split_axis=0, concat_axis=0, tiled=True)
    planes = (
        arrived.reshape(count_x, count_y, depth, cells_x, cells_y)
        .transpose(2, 0, 3, 1, 4)
        .reshape(depth, GRID_X, GRID_Y)
    )
    turn_x = halves(jnp.asarray(hartley(GRID_X)))
    turn_y = halves(jnp.asarray(hartley(GRID_Y)))
    volume = GRID_X * GRID_Y * GRID_Z * spacing**3
    column = green_factors(jnp.arange(GRID_X, dtype=jnp.int32), GRID_X).T
    row = green_factors(jnp.arange(GRID_Y, dtype=jnp.int32), GRID_Y)
    deep = green_factors(place * depth + jnp.arange(depth, dtype=jnp.int32), GRID_Z)
    deep = (deep * jnp.array([[1.0], [1.0 / (math.pi * volume)]], jnp.float32)).T[:, None, :]

    def whole(*shape):
        return pl.BlockSpec(shape, lambda k: (0,) * len(shape))

    plane = pl.BlockSpec((1, GRID_X, GRID_Y), lambda k: (k, 0, 0))
    waves = pl.pallas_call(
        wave_kernel,
        grid=(depth,),
        in_specs=[
            plane,
            whole(GRID_X, GRID_X),
            whole(GRID_X, GRID_X),
            whole(GRID_Y, GRID_Y),
            whole(GRID_Y, GRID_Y),
            whole(GRID_X, 2),
            whole(2, GRID_Y),
            pl.BlockSpec((1, 1, 2), lambda k: (k, 0, 0)),
        ],
        out_specs=plane,
        out_shape=jax.ShapeDtypeStruct((depth, GRID_X, GRID_Y), jnp.float32),
        name="waves",
    )(planes, *turn_x, *turn_y, column, row, deep)
    outgoing = (
        waves.reshape(depth, count_x, cells_x, count_y, cells_y)
        .transpose(1, 3, 0, 2, 4)
        .reshape(devices, depth, cells_x * cells_y)
    )
    arrived = lax.all_to_all(outgoing, ("gx", "gy"), split_axis=0, concat_axis=0, tiled=True)
    return jnp.transpose(arrived.reshape(GRID_Z, cells_x * cells_y)).reshape(
        cells_x, cells_y, GRID_Z
    )


def convolved_by_lines(charge_mesh, count_x, count_y):
    turn_x = jnp.asarray(hartley(GRID_X))
    turn_y = jnp.asarray(hartley(GRID_Y))
    product = functools.partial(
        jnp.einsum, precision=lax.Precision.HIGHEST, preferred_element_type=jnp.float32
    )
    exchange = functools.partial(lax.all_to_all, tiled=True)
    lines = exchange(charge_mesh, "gx", split_axis=2, concat_axis=0)
    lines = product("xyk,xu->uyk", lines, turn_x)
    lines = exchange(lines, "gy", split_axis=0, concat_axis=1)
    lines = product("uyk,yv->uvk", lines, turn_y)
    wide, _, depth = lines.shape
    start_x = lax.axis_index("gy") * wide
    start_z = lax.axis_index("gx") * depth
    volume = GRID_X * GRID_Y * GRID_Z * spacing**3
    fx = green_factors(start_x + jnp.arange(wide, dtype=jnp.int32), GRID_X)
    fy = green_factors(jnp.arange(GRID_Y, dtype=jnp.int32), GRID_Y)
    fz = green_factors(start_z + jnp.arange(depth, dtype=jnp.int32), GRID_Z)
    square = fx[0][:, None, None] + fy[0][:, None] + fz[0]
    scale = fx[1][:, None, None] * fy[1][:, None] * fz[1] / (math.pi * volume)
    lines = lines * jnp.where(square > 0.0, scale / jnp.where(square > 0.0, square, 1.0), 0.0)
    lines = product("uvk,vy->uyk", lines, turn_y)
    lines = exchange(lines, "gy", split_axis=1, concat_axis=0)
    lines = product("uyk,ux->xyk", lines, turn_x)
    return exchange(lines, "gx", split_axis=0, concat_axis=2)


def local(positions, charges, pair_lists, slab_dest, atom_counts):
    count_x = lax.axis_size("gx")
    count_y = lax.axis_size("gy")
    devices = count_x * count_y
    atom_total = positions.shape[3]
    clusters = pair_lists.shape[2]
    cluster_size = atom_total // clusters
    blocks = slab_dest.shape[2]
    block_size = atom_total // blocks
    cells_x = GRID_X // count_x
    cells_y = GRID_Y // count_y
    cells_z = GRID_Z // count_y
    living = jnp.arange(atom_total, dtype=jnp.int32) < atom_counts[0, 0]
    charge = jnp.where(living, charges[0, 0], 0.0)
    packed = jnp.concatenate([positions, charge[None, None, None, :]], axis=0)
    atoms = packed.reshape(4, atom_total)

    base = jnp.broadcast_to(
        (slab_dest[0, 0] * cells_z)[:, None], (blocks, block_size)
    ).reshape(1, atom_total)
    cells = (cells_x, cells_y, cells_z)
    pad = (round_up(cells_x + 3, rows_group), round_up(cells_y + 3, 8))
    pad_x, pad_y = pad
    turn_z = jnp.asarray(hartley(GRID_Z))
    spread = pl.pallas_call(
        functools.partial(spread_kernel, cells, pad),
        out_shape=jax.ShapeDtypeStruct((pad_x, pad_y, GRID_Z), jnp.float32),
        scratch_shapes=[
            pltpu.VMEM((pad_x, atom_total), jnp.float32),
            pltpu.VMEM((pad_y, atom_total), jnp.float32),
            pltpu.VMEM((atom_total, 2 * GRID_Z), jnp.bfloat16),
            pltpu.VMEM((rows_group * pad_y, atom_total), jnp.bfloat16),
            pltpu.VMEM((rows_group * pad_y, atom_total), jnp.bfloat16),
        ],
        name="spread",
    )(atoms, base, turn_z)

    from_x = moved(spread[cells_x : cells_x + 3, :cells_y], 1, 0)
    from_y = moved(spread[:cells_x, cells_y : cells_y + 3], 0, 1)
    from_both = moved(spread[cells_x : cells_x + 3, cells_y : cells_y + 3], 1, 1)
    charge_mesh = (
        spread[:cells_x, :cells_y]
        .at[:3]
        .add(from_x)
        .at[:, :3]
        .add(from_y)
        .at[:3, :3]
        .add(from_both)
    )
    by_planes = GRID_Z % devices == 0
    convolved = convolved_by_planes if by_planes else convolved_by_lines
    potential = convolved(charge_mesh, count_x, count_y)
    upper_x = moved(potential[:3], -1, 0)
    upper_y = moved(potential[:, :3], 0, -1)
    upper_both = moved(potential[:3, :3], -1, -1)
    wider = jnp.concatenate(
        [
            jnp.concatenate([potential, upper_x], axis=0),
            jnp.concatenate([upper_y, upper_both], axis=0),
        ],
        axis=1,
    )
    wider = jnp.pad(wider, ((0, pad_x - cells_x - 3), (0, pad_y - cells_y - 3), (0, 0)))
    far_part = pl.pallas_call(
        functools.partial(gather_kernel, cells, pad),
        out_shape=jax.ShapeDtypeStruct((3, atom_total), jnp.float32),
        scratch_shapes=[
            pltpu.VMEM((pad_x, atom_total), jnp.float32),
            pltpu.VMEM((pad_x, atom_total), jnp.float32),
            pltpu.VMEM((pad_y, atom_total), jnp.float32),
            pltpu.VMEM((pad_y, atom_total), jnp.float32),
            pltpu.VMEM((2 * GRID_Z, 2 * atom_total), jnp.bfloat16),
            pltpu.VMEM((rows_group * pad_y, 2 * atom_total), jnp.float32),
        ],
        name="gather",
    )(atoms, base, turn_z, wider)

    nearby = with_halo(packed, (("gx", 1), ("gy", 2)), 1)
    steps_x = (jnp.arange(3, dtype=jnp.float32) - 1.0) * cells_x
    steps_y = (jnp.arange(3, dtype=jnp.float32) - 1.0) * cells_y
    zero_grid = jnp.zeros((3, 3), jnp.float32)
    cell_shift = jnp.stack(
        [steps_x[:, None] + zero_grid, steps_y[None, :] + zero_grid, zero_grid, zero_grid]
    )
    beside_all = (nearby + cell_shift[:, :, :, None]).reshape(4, 9 * clusters, cluster_size)
    chosen = pair_lists[0, 0]
    pick = (chosen[:, :, None] == jnp.arange(9 * clusters, dtype=jnp.int32)).astype(jnp.float32)
    partners = jnp.einsum(
        "cln,fnk->cflk",
        pick,
        beside_all,
        precision=lax.Precision.HIGHEST,
        preferred_element_type=jnp.float32,
    ).reshape(clusters, 4, -1)
    own = packed.reshape(4, clusters, cluster_size)
    pair_part = jnp.stack(
        [one_cluster(own[:, c], partners[c]) for c in range(clusters)], axis=1
    )
    short_forces = pair_part.reshape(3, 1, 1, atom_total)
    return (short_forces, far_part.reshape(3, 1, 1, atom_total))


def solution(mesh):
    return jax.shard_map(
        local,
        mesh=mesh,
        in_specs=(
            P(None, ("rep", "gx"), "gy", None),
            P(("rep", "gx"), "gy", None),
            P(("rep", "gx"), "gy", None, None),
            P(("rep", "gx"), "gy", None),
            P(("rep", "gx"), "gy"),
        ),
        out_specs=(P(None, ("rep", "gx"), "gy", None), P(None, ("rep", "gx"), "gy", None)),
        check_vma=False,
    )
```

time: 625 us -> 215 us (0.34); the launches traced: 613 us -> 214 us
  local copies, waits for them, and re-layouts: 185 us -> 47.5 us
  matrix products: 129 us -> 0.25 us
  waiting for transfers between devices: 173 us -> 62.8 us
  other arithmetic: 71.1 us -> 24.6 us
  Pallas kernels: 0 us -> 40.3 us
  starting transfers between devices: 52.2 us -> 36.4 us
    dot_general x25 -> x1, matrix products: 129 us -> 0.25 us  [local(): jnp.einsum('cln,fnk->cflk', pick, beside_all, precision=lax.Precision.HIG...]
    all_to_all x10 -> x2, waiting for transfers between devices: 160 us -> 49.7 us  [convolved_by_planes(): lax.all_to_all(outgoing, ('gx', 'gy'), split_axis=0, concat_axis=0, tiled...]
    all_to_all x20 -> x0, local copies, waits for them, and re-layouts: 78.2 us -> none  [the longest x4 14.4 us: local(): lax.all_to_all(imag_part, 'gx', split_axis=2, concat_axis=0, tiled=True)]
    pallas_call x0 -> x3, Pallas kernels: none -> 40.3 us  [the longest x1 18 us: local(): pl.pallas_call(functools.partial(gather_kernel, cells, pad), out_shape=ja...]
    mul x2 -> x0, local copies, waits for them, and re-layouts: 38.6 us -> none  [local(): mesh_atoms[3][:, None, None] * weight_x[:, :, None] * weight_z[:, None, :]]
    unnamed x89 -> x26, local copies, waits for them, and re-layouts: 40.1 us -> 4.58 us
    all_to_all x4 -> x0, other arithmetic: 30.8 us -> none  [the longest x1 7.69 us: local(): lax.all_to_all(imag_part, 'gx', split_axis=2, concat_axis=0, tiled=True)]
    all_to_all x10 -> x2, starting transfers between devices: 43.6 us -> 16.1 us  [convolved_by_planes(): lax.all_to_all(outgoing, ('gx', 'gy'), split_axis=0, concat_axis=0, tiled...]
  transfers between devices with their start and end apart: 18 -> 12, of which waited for: 12 -> 6; matrix products, arithmetic and copies ran while one was open for 29% -> 15% of each run, Pallas kernels for 0% -> 5%
where the time goes in v1:
time: 215 us; the launch traced here: 214 us
  waiting for transfers between devices  62.8 us (29%)
  local copies, waits for them, and re-layouts  47.5 us (22%)
  Pallas kernels  40.3 us (19%)
  starting transfers between devices  36.4 us (17%)
  other arithmetic  24.6 us (11%)
    all_to_all x2, waiting for transfers between devices, convolved_by_planes(): lax.all_to_all(outgoing, ('gx', 'gy'), split_axis=0, concat_axis=0, tiled...  49.7 us
    pallas_call x1, Pallas kernels, local(): pl.pallas_call(functools.partial(gather_kernel, cells, pad), out_shape=ja...  18 us
    all_to_all x2, starting transfers between devices, convolved_by_planes(): lax.all_to_all(outgoing, ('gx', 'gy'), split_axis=0, concat_axis=0, tiled...  16.1 us
    ppermute x6, starting transfers between devices, moved(): return lax.ppermute(value, ('gx', 'gy'), pairs)  13.4 us
    mul x8, other arithmetic, one_cluster(): return own_rows[3] * jnp.sum(weight[None] * offsets, axis=2)  13.3 us
    pallas_call x1, Pallas kernels, convolved_by_planes(): pl.pallas_call(wave_kernel, grid=(depth,), in_specs=[plane, whole(GRID_X,...  11.6 us
    pallas_call x1, Pallas kernels, local(): pl.pallas_call(functools.partial(spread_kernel, cells, pad), out_shape=ja...  10.7 us
    reshape x2, local copies, waits for them, and re-layouts, convolved_by_planes(): waves.reshape(depth, count_x, cells_x, count_y, cells_y)  9.8 us
  transfers between devices with their start and end apart: 12, of which 6 were waited for; matrix products, arithmetic and copies ran while one was open for 15% of the time, Pallas kernels for 5%

profile of v1, /device:TPU:0, one launch (start us, length us, event | category | flops | bytes accessed | tf_op | source)
XLA Modules:
  0.0 213.6 jit_solution(15985029355059434961)
XLA Ops:
  2.7 5.1 %collective-permute-start.1 = (f32[4,1,1,1024]{3,0,2,1:T(4,128)S(1)}, f32[4,1,1,1024]{3,0,2,1:T(4,128)S(1)}, u32[]{:S(2)}, u32[]{:S(2)}) collective-permute-start(f32[4,1,1,1024]{3,0,2,1:T(4,128)S(1)} %pad_maximum_fusion.1), channel_id=1, source_target_pairs={{4,0},{8,4},{12,8},{0,12},{5,1},{9,5},{13,9},{1,13},{6,2},{10,6},{... | collective-permute-start | bytes 49160 | tf_op jit(solution)/shard_map/ppermute | solution.py:33
  9.8 10.7 %spread.1 = f32[72,72,128]{2,1,0:T(8,128)} custom-call(f32[4,1024]{1,0:T(4,128)} %fusion.77.atoms_ref, s32[1,1024]{1,0:T(1,128)} %bitcast.118, f32[128,128]{1,0:T(8,128)} %constant.212.clone.turn_ref), custom_call_target="tpu_custom_call" | custom-call | tf_op jit(solution)/shard_map/spread/pallas_call | solution.py:340
  23.2 2.8 %collective-permute-start.6 = (f32[3,3,128]{2,1,0:T(4,128)S(1)}, f32[3,3,128]{2,1,0:T(4,128)S(1)}, u32[]{:S(2)}, u32[]{:S(2)}) collective-permute-start(f32[3,3,128]{2,1,0:T(4,128)S(1)} %slice.251), channel_id=1, source_target_pairs={{0,5},{1,6},{2,7},{3,4},{4,9},{5,10},{6,11},{7,8},{8,13},{9,14},{1... | collective-permute-start | bytes 13832 | tf_op jit(solution)/shard_map/ppermute | solution.py:46
  32.8 4.9 %all-to-all-start = ((f32[16,8,4096]{2,1,0:T(8,128)}), f32[16,8,4096]{2,1,0:T(8,128)S(1)}, u32[]{:S(2)}, u32[]{:S(2)}) async-start(f32[16,8,4096]{2,1,0:T(8,128)} %bitcast.106), calls=%async_computation | async-start | bytes 4194304 | tf_op jit(solution)/shard_map/all_to_all | solution.py:243
  41.6 6.6 %collective-permute-done.3 = f32[4,3,1,1024]{3,0,2,1:T(4,128)S(1)} collective-permute-done((f32[4,3,1,1024]{3,0,2,1:T(4,128)S(1)}, f32[4,3,1,1024]{3,0,2,1:T(4,128)S(1)}, u32[]{:S(2)}, u32[]{:S(2)}) %collective-permute-start.3) | collective-permute-done | bytes 49184 | tf_op jit(solution)/shard_map/ppermute | solution.py:33
  48.1 2.6 %collective-permute-done.2 = f32[4,3,1,1024]{3,0,2,1:T(4,128)S(1)} collective-permute-done((f32[4,3,1,1024]{3,0,2,1:T(4,128)S(1)}, f32[4,3,1,1024]{3,0,2,1:T(4,128)S(1)}, u32[]{:S(2)}, u32[]{:S(2)}) %collective-permute-start.2) | collective-permute-done | bytes 49184 | tf_op jit(solution)/shard_map/ppermute | solution.py:32
  52.4 4.1 %multiply_multiply_fusion = f32[256,1024]{1,0:T(8,128)} fusion(f32[256,1024]{1,0:T(8,128)S(1)} %fusion.10, f32[1024]{0:T(1024)S(1)} %bitcast.122), kind=kLoop, calls=%fused_computation.59 | loop fusion | flops 19922944 | bytes 2101248 | tf_op jit(solution)/shard_map/mul | solution.py:232
  56.4 3.0 %multiply_multiply_fusion.2 = f32[256,1024]{1,0:T(8,128)S(1)} fusion(f32[256,1024]{1,0:T(8,128)S(1)} %fusion.7, f32[1024]{0:T(1024)S(1)} %bitcast.123), kind=kLoop, calls=%fused_computation.69 | loop fusion | flops 19922944 | bytes 2101248 | tf_op jit(solution)/shard_map/mul | solution.py:232
  59.5 19.1 %all-to-all-done = f32[16,8,4096]{2,1,0:T(8,128)S(1)} async-done(((f32[16,8,4096]{2,1,0:T(8,128)}), f32[16,8,4096]{2,1,0:T(8,128)S(1)}, u32[]{:S(2)}, u32[]{:S(2)}) %all-to-all-start) | async-done | bytes 2097184 | tf_op jit(solution)/shard_map/all_to_all | solution.py:243
  78.6 3.0 %reshape.899 = f32[4,4,8,64,64]{4,3,2,1,0:T(8,128)} reshape(f32[16,8,4096]{2,1,0:T(8,128)S(1)} %all-to-all-done) | data formatting | bytes 4194304 | tf_op jit(solution)/shard_map/reshape | solution.py:245
  81.6 7.7 %copy.38 = f32[8,4,64,4,64]{4,3,2,1,0:T(4,128)} copy(f32[8,4,64,4,64]{4,2,0,3,1:T(8,128)} %bitcast.98) | data formatting | bytes 4194304 | tf_op jit(solution)/shard_map/transpose | solution.py:246
  89.3 5.3 %reshape.900.mesh_ref = f32[8,256,256]{2,1,0:T(8,128)} reshape(f32[8,4,64,4,64]{4,3,2,1,0:T(4,128)} %copy.38) | data formatting | bytes 4194304 | tf_op jit(solution)/shard_map/reshape | solution.py:247
  94.6 11.6 %waves.1 = f32[8,256,256]{2,1,0:T(8,128)} custom-call(f32[8,256,256]{2,1,0:T(8,128)} %reshape.900.mesh_ref, bf16[256,256]{1,0:T(8,128)(2,1)} %constant.222.xh_ref.yh_ref, bf16[256,256]{1,0:T(8,128)(2,1)} %constant.225.xl_ref.yl_ref, bf16[256,256]{1,0:T(8,128)(2,1)} %constant.222.xh_ref.yh_ref, bf16[256,256]{1,0:T(8,128)(2,1)} %constant.225.xl_ref.yl_ref, ...), custom_call_target="tpu_custom_call" | custom-call | tf_op jit(solution)/shard_map/waves/pallas_call | solution.py:261
  106.2 5.1 %reshape.901 = f32[8,4,64,4,64]{4,3,2,1,0:T(4,128)} reshape(f32[8,256,256]{2,1,0:T(8,128)} %waves.1) | data formatting | bytes 4194304 | tf_op jit(solution)/shard_map/reshape | solution.py:279
  111.3 4.7 %copy.64 = f32[8,4,64,4,64]{4,2,0,3,1:T(8,128)} copy(f32[8,4,64,4,64]{4,3,2,1,0:T(4,128)} %reshape.901) | data formatting | bytes 4194304 | tf_op jit(solution)/shard_map/reshape | solution.py:279
  116.0 4.8 %reshape.902 = f32[16,8,4096]{2,1,0:T(8,128)} reshape(f32[4,4,8,64,64]{4,3,2,1,0:T(8,128)} %bitcast.99) | data formatting | bytes 4194304 | tf_op jit(solution)/shard_map/reshape | solution.py:281
  120.8 11.3 %all-to-all-start.1 = ((f32[16,8,4096]{2,1,0:T(8,128)}), f32[16,8,4096]{2,1,0:T(8,128)S(1)}, u32[]{:S(2)}, u32[]{:S(2)}) async-start(f32[16,8,4096]{2,1,0:T(8,128)} %reshape.902), calls=%async_computation.1 | async-start | bytes 4194304 | tf_op jit(solution)/shard_map/all_to_all | solution.py:283
  135.2 3.1 %multiply_multiply_fusion.4 = f32[256,1024]{1,0:T(8,128)S(1)} fusion(f32[256,1024]{1,0:T(8,128)S(1)} %fusion.4, f32[1024]{0:T(1024)S(1)} %bitcast.120), kind=kLoop, calls=%fused_computation.79 | loop fusion | flops 19922944 | bytes 2101248 | tf_op jit(solution)/shard_map/mul | solution.py:232
  138.8 3.1 %multiply_multiply_fusion.6 = f32[256,1024]{1,0:T(8,128)S(1)} fusion(f32[256,1024]{1,0:T(8,128)S(1)} %fusion.1, f32[1024]{0:T(1024)S(1)} %bitcast.121), kind=kLoop, calls=%fused_computation.89 | loop fusion | flops 19922944 | bytes 2101248 | tf_op jit(solution)/shard_map/mul | solution.py:232
  142.5 30.6 %all-to-all-done.1 = f32[16,8,4096]{2,1,0:T(8,128)S(1)} async-done(((f32[16,8,4096]{2,1,0:T(8,128)}), f32[16,8,4096]{2,1,0:T(8,128)S(1)}, u32[]{:S(2)}, u32[]{:S(2)}) %all-to-all-start.1) | async-done | bytes 2097184 | tf_op jit(solution)/shard_map/all_to_all | solution.py:283
  174.4 1.9 copy.42
  177.3 9.9 %collective-permute-start.9 = (f32[3,3,128]{2,1,0:T(4,128)S(1)}, f32[3,3,128]{2,1,0:T(4,128)S(1)}, u32[]{:S(2)}, u32[]{:S(2)}) collective-permute-start(f32[3,3,128]{2,1,0:T(4,128)S(1)} %slice.254), channel_id=1, source_target_pairs={{0,15},{1,12},{2,13},{3,14},{4,3},{5,0},{6,1},{7,2},{8,7},{9,4},{1... | collective-permute-start | bytes 13832 | tf_op jit(solution)/shard_map/ppermute | solution.py:46
  190.0 2.6 %collective-permute-done.7 = f32[3,64,128]{2,1,0:T(8,128)S(1)} collective-permute-done((f32[3,64,128]{2,1,0:T(8,128)S(1)}, f32[3,64,128]{2,1,0:T(8,128)S(1)}, u32[]{:S(2)}, u32[]{:S(2)}) %collective-permute-start.7) | collective-permute-done | bytes 98336 | tf_op jit(solution)/shard_map/ppermute | solution.py:46
  194.3 18.0 %gather.1 = f32[3,1024]{1,0:T(4,128)} custom-call(f32[4,1024]{1,0:T(4,128)} %fusion.77.atoms_ref, s32[1,1024]{1,0:T(1,128)} %bitcast.119, f32[128,128]{1,0:T(8,128)} %constant.212.clone.turn_ref, f32[72,72,128]{2,1,0:T(8,128)} %fusion.12.mesh_ref), custom_call_target="tpu_custom_call" | custom-call | tf_op jit(solution)/shard_map/gather/pallas_call | solution.py:379
  (97 shorter events, 30.4 us)
Async XLA Ops:
  2.7 35.1 %collective-permute-start.1 = (f32[4,1,1,1024]{3,0,2,1:T(4,128)S(1)}, f32[4,1,1,1024]{3,0,2,1:T(4,128)S(1)}, u32[]{:S(2)}, u32[]{:S(2)}) collective-permute-start(f32[4,1,1,1024]{3,0,2,1:T(4,128)S(1)} %pad_maximum_fusion.1), channel_id=1, source_target_pairs={{4,0},{8,4},{12,8},{0,12},{5,1},{9,5},{13,9},{1,13},{6,2},{10,6},{... | collective-permute-start | bytes 49160 | tf_op jit(solution)/shard_map/ppermute | solution.py:33
  7.8 30.0 %collective-permute-start = (f32[4,1,1,1024]{3,0,2,1:T(4,128)S(1)}, f32[4,1,1,1024]{3,0,2,1:T(4,128)S(1)}, u32[]{:S(2)}, u32[]{:S(2)}) collective-permute-start(f32[4,1,1,1024]{3,0,2,1:T(4,128)S(1)} %pad_maximum_fusion.1), channel_id=1, source_target_pairs={{0,4},{4,8},{8,12},{12,0},{1,5},{5,9},{9,13},{13,1},{2,6},{6,10},{... | collective-permute-start | bytes 49160 | tf_op jit(solution)/shard_map/ppermute | solution.py:32
  9.8 17.9 %copy-start.1 = (f32[3,1,1,1024]{3,2,1,0:T(1,128)S(1)}, f32[3,1,1,1024]{3,2,1,0:T(1,128)}, u32[]{:S(2)}) copy-start(f32[3,1,1,1024]{3,2,1,0:T(1,128)} %param.15) | copy-start | bytes 36868
  9.8 18.5 %copy-start.2 = (f32[1,1,1024]{2,1,0:T(1,128)S(1)}, f32[1,1,1024]{2,1,0:T(1,128)}, u32[]{:S(2)}) copy-start(f32[1,1,1024]{2,1,0:T(1,128)} %param.16) | copy-start | bytes 12292
  21.4 7.9 %collective-permute-start.4 = (f32[3,64,128]{2,1,0:T(8,128)S(1)}, f32[3,64,128]{2,1,0:T(8,128)S(1)}, u32[]{:S(2)}, u32[]{:S(2)}) collective-permute-start(f32[3,64,128]{2,1,0:T(8,128)S(1)} %slice.247), channel_id=1, source_target_pairs={{0,4},{1,5},{2,6},{3,7},{4,8},{5,9},{6,10},{7,11},{8,12},{9,13},{1... | collective-permute-start | bytes 294920 | tf_op jit(solution)/shard_map/ppermute | solution.py:46
  22.4 7.8 %collective-permute-start.5 = (f32[64,3,128]{2,1,0:T(4,128)S(1)}, f32[64,3,128]{2,1,0:T(4,128)S(1)}, u32[]{:S(2)}, u32[]{:S(2)}) collective-permute-start(f32[64,3,128]{2,1,0:T(4,128)S(1)} %slice.249), channel_id=1, source_target_pairs={{0,1},{1,2},{2,3},{3,0},{4,5},{5,6},{6,7},{7,4},{8,9},{9,10},{10,1... | collective-permute-start | bytes 294920 | tf_op jit(solution)/shard_map/ppermute | solution.py:46
  23.2 7.6 %collective-permute-start.6 = (f32[3,3,128]{2,1,0:T(4,128)S(1)}, f32[3,3,128]{2,1,0:T(4,128)S(1)}, u32[]{:S(2)}, u32[]{:S(2)}) collective-permute-start(f32[3,3,128]{2,1,0:T(4,128)S(1)} %slice.251), channel_id=1, source_target_pairs={{0,5},{1,6},{2,7},{3,4},{4,9},{5,10},{6,11},{7,8},{8,13},{9,14},{1... | collective-permute-start | bytes 13832 | tf_op jit(solution)/shard_map/ppermute | solution.py:46
  32.8 4.9 %copy-start.4 = (f32[2]{0:T(128)S(1)}, f32[2]{0:T(128)}, u32[]{:S(2)}) copy-start(f32[2]{0:T(128)} %constant.226) | copy-start | bytes 28
  32.8 18.3 %copy-start.3 = (s32[1,1,4,4]{3,2,1,0:T(4,128)S(1)}, s32[1,1,4,4]{3,2,1,0:T(4,128)}, u32[]{:S(2)}) copy-start(s32[1,1,4,4]{3,2,1,0:T(4,128)} %param.17) | copy-start | bytes 196
  32.8 45.8 %all-to-all-start = ((f32[16,8,4096]{2,1,0:T(8,128)}), f32[16,8,4096]{2,1,0:T(8,128)S(1)}, u32[]{:S(2)}, u32[]{:S(2)}) async-start(f32[16,8,4096]{2,1,0:T(8,128)} %bitcast.106), calls=%async_computation | async-start | bytes 4194304 | tf_op jit(solution)/shard_map/all_to_all | solution.py:243
  37.8 10.3 %collective-permute-start.3 = (f32[4,3,1,1024]{3,0,2,1:T(4,128)S(1)}, f32[4,3,1,1024]{3,0,2,1:T(4,128)S(1)}, u32[]{:S(2)}, u32[]{:S(2)}) collective-permute-start(f32[4,3,1,1024]{3,0,2,1:T(4,128)S(1)} %pad_maximum_fusion), channel_id=1, source_target_pairs={{1,0},{2,1},{3,2},{0,3},{5,4},{6,5},{7,6},{4,7},{9,8},{10,9},{11,1... | collective-permute-start | bytes 147464 | tf_op jit(solution)/shard_map/ppermute | solution.py:33
  39.5 11.3 %collective-permute-start.2 = (f32[4,3,1,1024]{3,0,2,1:T(4,128)S(1)}, f32[4,3,1,1024]{3,0,2,1:T(4,128)S(1)}, u32[]{:S(2)}, u32[]{:S(2)}) collective-permute-start(f32[4,3,1,1024]{3,0,2,1:T(4,128)S(1)} %pad_maximum_fusion), channel_id=1, source_target_pairs={{0,1},{1,2},{2,3},{3,0},{4,5},{5,6},{6,7},{7,4},{8,9},{9,10},{10,1... | collective-permute-start | bytes 147464 | tf_op jit(solution)/shard_map/ppermute | solution.py:32
  120.8 52.2 %all-to-all-start.1 = ((f32[16,8,4096]{2,1,0:T(8,128)}), f32[16,8,4096]{2,1,0:T(8,128)S(1)}, u32[]{:S(2)}, u32[]{:S(2)}) async-start(f32[16,8,4096]{2,1,0:T(8,128)} %reshape.902), calls=%async_computation.1 | async-start | bytes 4194304 | tf_op jit(solution)/shard_map/all_to_all | solution.py:283
  173.0 1.4 copy-start
  177.3 11.3 %collective-permute-start.9 = (f32[3,3,128]{2,1,0:T(4,128)S(1)}, f32[3,3,128]{2,1,0:T(4,128)S(1)}, u32[]{:S(2)}, u32[]{:S(2)}) collective-permute-start(f32[3,3,128]{2,1,0:T(4,128)S(1)} %slice.254), channel_id=1, source_target_pairs={{0,15},{1,12},{2,13},{3,14},{4,3},{5,0},{6,1},{7,2},{8,7},{9,4},{1... | collective-permute-start | bytes 13832 | tf_op jit(solution)/shard_map/ppermute | solution.py:46
  187.2 2.8 %collective-permute-start.8 = (f32[64,3,128]{2,1,0:T(4,128)S(1)}, f32[64,3,128]{2,1,0:T(4,128)S(1)}, u32[]{:S(2)}, u32[]{:S(2)}) collective-permute-start(f32[64,3,128]{2,1,0:T(4,128)S(1)} %slice.253), channel_id=1, source_target_pairs={{0,3},{1,0},{2,1},{3,2},{4,7},{5,4},{6,5},{7,6},{8,11},{9,8},{10,9... | collective-permute-start | bytes 294920 | tf_op jit(solution)/shard_map/ppermute | solution.py:46
  187.5 5.0 %collective-permute-start.7 = (f32[3,64,128]{2,1,0:T(8,128)S(1)}, f32[3,64,128]{2,1,0:T(8,128)S(1)}, u32[]{:S(2)}, u32[]{:S(2)}) collective-permute-start(f32[3,64,128]{2,1,0:T(8,128)S(1)} %bitcast.115), channel_id=1, source_target_pairs={{0,12},{1,13},{2,14},{3,15},{4,0},{5,1},{6,2},{7,3},{8,4},{9,5},{1... | collective-permute-start | bytes 294920 | tf_op jit(solution)/shard_map/ppermute | solution.py:46

commit v2 on v1

--- a/solution.py
+++ b/solution.py
@@ -20,19 +20,6 @@
 soft_core = 0.09
 root_factor = 1.1283791670955126
 rows_group = 8
-
-
-def with_halo(value, sides, width):
-    for axis, dim in sides:
-        count, length = (lax.axis_size(axis), value.shape[dim])
-        up = [(i, (i + 1) % count) for i in range(count)]
-        down = [(j, i) for i, j in up]
-        last = lax.slice_in_dim(value, length - width, length, axis=dim)
-        initial = lax.slice_in_dim(value, 0, width, axis=dim)
-        before = lax.ppermute(last, axis, up)
-        after = lax.ppermute(initial, axis, down)
-        value = jnp.concatenate([before, value, after], axis=dim)
-    return value
 
 
 def moved(value, step_x, step_y):
@@ -190,7 +177,75 @@
         out_ref[pl.ds(place, 1), :] = factor * jnp.sum(sums[place], axis=0, keepdims=True)
 
 
-def wave_kernel(mesh_ref, xh_ref, xl_ref, yh_ref, yl_ref, column_ref, row_ref, depth_ref, out_ref):
+def depth_rows(table, height, fraction, terms):
+    turns = (height * table[:, 0:1]).astype(jnp.int32) % GRID_Z
+    phases = turns.astype(jnp.float32) * (2.0 * math.pi / GRID_Z)
+    cosine, sine = (jnp.cos(phases), jnp.sin(phases))
+    results = []
+    for weights in terms:
+        even = sum(table[:, 1 + t : 2 + t] * weights[t] for t in range(4))
+        odd = sum(table[:, 5 + t : 6 + t] * weights[t] for t in range(4))
+        results.append(cosine * even + sine * odd)
+    return results
+
+
+def mesh_kernel(sizes, cells, pad, atoms_ref, xh_ref, xl_ref, yh_ref, yl_ref, column_ref, row_ref, depth_ref, table_ref, out_ref, wx_ref, vx_ref, wy_ref, hi_ref, lo_ref, mesh_ref, turned_ref, level_ref, stack_ref, side_ref):
+    count_x, count_y = sizes
+    cells_x, cells_y = cells
+    pad_x, pad_y = pad
+    atom_total = atoms_ref.shape[2]
+    depth = depth_ref.shape[0]
+    window = 2 * cells_y
+    windows = GRID_Y // window
+    lane = lax.broadcasted_iota(jnp.int32, (depth * pad_x, window), 1)
+    mesh_ref[...] = jnp.zeros_like(mesh_ref)
+    wy_ref[...] = jnp.zeros_like(wy_ref)
+    table = table_ref[...]
+
+    def atoms_of(cell, row):
+        return atoms_ref[cell, row : row + 1, :]
+
+    def spread_cell(cell, i, j):
+        low_x, frac_x = split_cells(atoms_of(cell, 0), 0.0, cells_x)
+        low_y, frac_y = split_cells(atoms_of(cell, 1), 0.0, cells_y)
+        wx_ref[...] = spline_table(low_x, spline_weights(frac_x)[0], pad_x)
+        high, low = halves(spline_table(low_y, spline_weights(frac_y)[0], pad_y))
+        wy_ref[:pad_y, :] = high
+        wy_ref[pl.ds(window, pad_y), :] = low
+        frac_z = atoms_of(cell, 5)
+        (deep,) = depth_rows(table, atoms_of(cell, 4), frac_z, [spline_weights(frac_z)[0]])
+        deep = deep * atoms_of(cell, 3)
+        for k in range(depth):
+            high, low = halves(deep[k : k + 1, :] * wx_ref[...])
+            hi_ref[pl.ds(k * pad_x, pad_x), :] = high
+            lo_ref[pl.ds(k * pad_x, pad_x), :] = low
+        numbers = (((1,), (1,)), ((), ()))
+        both = lax.dot_general(
+            hi_ref[...], wy_ref[...], numbers, preferred_element_type=jnp.float32
+        )
+        rest = lax.dot_general(
+            lo_ref[...], wy_ref[:window, :], numbers, preferred_element_type=jnp.float32
+        )
+        total = both[:, :window] + both[:, window:] + rest
+        rows = pl.ds(pl.multiple_of(i * cells_x, 8), pad_x)
+        m = j // 2
+        if j % 2 == 0:
+            mesh_ref[:, rows, pl.ds(m * window, window)] += total.reshape(depth, pad_x, window)
+        else:
+            total = pltpu.roll(total, cells_y, 1)
+            kept = jnp.where(lane >= cells_y, total, 0.0)
+            carried = jnp.where(lane < cells_y, total, 0.0)
+            after = (m + 1) % windows
+            mesh_ref[:, rows, pl.ds(m * window, window)] += kept.reshape(depth, pad_x, window)
+            mesh_ref[:, rows, pl.ds(after * window, window)] += carried.reshape(
+                depth, pad_x, window
+            )
+
+    @pl.loop(0, count_x)
+    def _(i):
+        for j in range(count_y):
+            spread_cell(i * count_y + j, i, j)
+
     def across(value):
         high, low = halves(value)
         return dot(xh_ref[...], high) + dot(xl_ref[...], high) + dot(xh_ref[...], low)
@@ -199,11 +254,70 @@
         high, low = halves(value)
         return dot(high, yh_ref[...]) + dot(high, yl_ref[...]) + dot(low, yh_ref[...])
 
-    waves = along(across(mesh_ref[0]))
-    square = column_ref[:, 0:1] + row_ref[0:1, :] + depth_ref[0, 0:1, 0:1]
-    scale = column_ref[:, 1:2] * row_ref[1:2, :] * depth_ref[0, 0:1, 1:2]
-    green = jnp.where(square > 0.0, scale / jnp.where(square > 0.0, square, 1.0), 0.0)
-    out_ref[0] = across(along(waves * green))
+    extra = mesh_ref.shape[1] - GRID_X
+
+    @pl.loop(0, depth)
+    def _(k):
+        mesh_ref[k, :extra, :] += mesh_ref[k, GRID_X:, :]
+        waves = along(across(mesh_ref[k, :GRID_X, :]))
+        square = column_ref[:, 0:1] + row_ref[0:1, :] + depth_ref[k, 0:1, 0:1]
+        scale = column_ref[:, 1:2] * row_ref[1:2, :] * depth_ref[k, 0:1, 1:2]
+        green = jnp.where(square > 0.0, scale / jnp.where(square > 0.0, square, 1.0), 0.0)
+        plane = across(along(waves * green))
+        mesh_ref[k, :GRID_X, :] = plane
+        mesh_ref[k, GRID_X:, :] = plane[:extra]
+        rolled = pltpu.roll(plane, GRID_Y - cells_y, 1)
+        turned_ref[k, :GRID_X, :] = rolled
+        turned_ref[k, GRID_X:, :] = rolled[:extra]
+
+    stride = round_up(pad_y, 16)
+    side_ref[...] = jnp.zeros_like(side_ref)
+    groups = pad_x // 8
+
+    def gather_cell(cell, i, j):
+        low_x, frac_x = split_cells(atoms_of(cell, 0), 0.0, cells_x)
+        low_y, frac_y = split_cells(atoms_of(cell, 1), 0.0, cells_y)
+        values, slopes = spline_weights(frac_x)
+        wx_ref[...] = spline_table(low_x, values, pad_x)
+        vx_ref[...] = spline_table(low_x, slopes, pad_x)
+        for place, terms in enumerate(spline_weights(frac_y)):
+            high, low = halves(spline_table(low_y, terms, stride))
+            span = pl.ds(place * atom_total, atom_total)
+            side_ref[:stride, span] = high
+            side_ref[pl.ds(stride, stride), span] = low
+            side_ref[pl.ds(2 * stride, stride), span] = high
+        frac_z = atoms_of(cell, 5)
+        deep, steep = depth_rows(table, atoms_of(cell, 4), frac_z, spline_weights(frac_z))
+        source = mesh_ref if j % 2 == 0 else turned_ref
+        rows = pl.ds(pl.multiple_of(i * cells_x, 8), pad_x)
+        block = source[:, rows, pl.ds(j // 2 * window, window)].reshape(depth * pad_x, window)
+        high = block.astype(jnp.bfloat16).astype(jnp.float32)
+        low = block - high
+        shifted = pltpu.roll(high, stride, 1)
+        stack_ref[:, :window] = jnp.where(lane < stride, high, shifted).astype(jnp.bfloat16)
+        stack_ref[:, window:] = jnp.where(
+            lane < 2 * stride - window, shifted, pltpu.roll(low, 2 * stride - window, 1)
+        ).astype(jnp.bfloat16)
+        level_ref[...] = dot(stack_ref[...], side_ref[...])
+        zero = jnp.zeros((8, atom_total), jnp.float32)
+        first, second, third = (zero, zero, zero)
+        for k in range(depth):
+            flat = level_ref[pl.ds(k * pad_x, pad_x), :atom_total]
+            tilt = level_ref[pl.ds(k * pad_x, pad_x), atom_total:]
+            weight = wx_ref[...]
+            part_x = jnp.sum((vx_ref[...] * flat).reshape(groups, 8, atom_total), axis=0)
+            part_y = jnp.sum((weight * tilt).reshape(groups, 8, atom_total), axis=0)
+            part_z = jnp.sum((weight * flat).reshape(groups, 8, atom_total), axis=0)
+            first = first + deep[k : k + 1, :] * part_x
+            second = second + deep[k : k + 1, :] * part_y
+            third = third + steep[k : k + 1, :] * part_z
+        for place, value in enumerate((first, second, third)):
+            out_ref[cell, pl.ds(place, 1), :] = jnp.sum(value, axis=0, keepdims=True)
+
+    @pl.loop(0, count_x)
+    def _(i):
+        for j in range(count_y):
+            gather_cell(i * count_y + j, i, j)
 
 
 def green_factors(index, period):
@@ -232,58 +346,58 @@
     return own_rows[3] * jnp.sum(weight[None] * offsets, axis=2)
 
 
-def convolved_by_planes(charge_mesh, count_x, count_y):
-    cells_x, cells_y = charge_mesh.shape[:2]
+def far_by_planes(gathered, own_charge, count_x, count_y, cells_x, cells_y):
     devices = count_x * count_y
     place = lax.axis_index("gx") * count_y + lax.axis_index("gy")
     depth = GRID_Z // devices
-    outgoing = jnp.transpose(charge_mesh.reshape(cells_x * cells_y, GRID_Z)).reshape(
-        devices, depth, cells_x * cells_y
-    )
-    arrived = lax.all_to_all(outgoing, ("gx", "gy"), split_axis=0, concat_axis=0, tiled=True)
-    planes = (
-        arrived.reshape(count_x, count_y, depth, cells_x, cells_y)
-        .transpose(2, 0, 3, 1, 4)
-        .reshape(depth, GRID_X, GRID_Y)
-    )
+    atom_total = gathered.shape[2]
+    pad_x = round_up(cells_x + 3, 8)
+    pad_y = round_up(cells_y + 3, 8)
+    window = 2 * cells_y
     turn_x = halves(jnp.asarray(hartley(GRID_X)))
     turn_y = halves(jnp.asarray(hartley(GRID_Y)))
     volume = GRID_X * GRID_Y * GRID_Z * spacing**3
     column = green_factors(jnp.arange(GRID_X, dtype=jnp.int32), GRID_X).T
     row = green_factors(jnp.arange(GRID_Y, dtype=jnp.int32), GRID_Y)
-    deep = green_factors(place * depth + jnp.arange(depth, dtype=jnp.int32), GRID_Z)
+    own_k = place * depth + jnp.arange(depth, dtype=jnp.int32)
+    deep = green_factors(own_k, GRID_Z)
     deep = (deep * jnp.array([[1.0], [1.0 / (math.pi * volume)]], jnp.float32)).T[:, None, :]
-
-    def whole(*shape):
-        return pl.BlockSpec(shape, lambda k: (0,) * len(shape))
-
-    plane = pl.BlockSpec((1, GRID_X, GRID_Y), lambda k: (k, 0, 0))
-    waves = pl.pallas_call(
-        wave_kernel,
-        grid=(depth,),
-        in_specs=[
-            plane,
-            whole(GRID_X, GRID_X),
-            whole(GRID_X, GRID_X),
-            whole(GRID_Y, GRID_Y),
-            whole(GRID_Y, GRID_Y),
-            whole(GRID_X, 2),
-            whole(2, GRID_Y),
-            pl.BlockSpec((1, 1, 2), lambda k: (k, 0, 0)),
+    taps = (own_k[:, None] * jnp.arange(4, dtype=jnp.int32)).astype(jnp.float32)
+    taps = taps * (2.0 * math.pi / GRID_Z)
+    cosine, sine = (jnp.cos(taps), jnp.sin(taps))
+    table = jnp.concatenate(
+        [own_k[:, None].astype(jnp.float32), cosine + sine, cosine - sine], axis=1
+    )
+    vmem = pl.BlockSpec(memory_space=pltpu.VMEM)
+    rows = GRID_X + pad_x - cells_x
+    partial = pl.pallas_call(
+        functools.partial(mesh_kernel, (count_x, count_y), (cells_x, cells_y), (pad_x, pad_y)),
+        in_specs=[vmem] * 9,
+        out_specs=vmem,
+        out_shape=jax.ShapeDtypeStruct((devices, 3, atom_total), jnp.float32),
+        scratch_shapes=[
+            pltpu.VMEM((pad_x, atom_total), jnp.float32),
+            pltpu.VMEM((pad_x, atom_total), jnp.float32),
+            pltpu.VMEM((2 * window, atom_total), jnp.bfloat16),
+            pltpu.VMEM((depth * pad_x, atom_total), jnp.bfloat16),
+            pltpu.VMEM((depth * pad_x, atom_total), jnp.bfloat16),
+            pltpu.VMEM((depth, rows, GRID_Y), jnp.float32),
+            pltpu.VMEM((depth, rows, GRID_Y), jnp.float32),
+            pltpu.VMEM((depth * pad_x, 2 * atom_total), jnp.float32),
+            pltpu.VMEM((depth * pad_x, 2 * window), jnp.bfloat16),
+            pltpu.VMEM((2 * window, 2 * atom_total), jnp.bfloat16),
         ],
-        out_specs=plane,
-        out_shape=jax.ShapeDtypeStruct((depth, GRID_X, GRID_Y), jnp.float32),
-        name="waves",
-    )(planes, *turn_x, *turn_y, column, row, deep)
-    outgoing = (
-        waves.reshape(depth, count_x, cells_x, count_y, cells_y)
-        .transpose(1, 3, 0, 2, 4)
-        .reshape(devices, depth, cells_x * cells_y)
-    )
-    arrived = lax.all_to_all(outgoing, ("gx", "gy"), split_axis=0, concat_axis=0, tiled=True)
-    return jnp.transpose(arrived.reshape(GRID_Z, cells_x * cells_y)).reshape(
-        cells_x, cells_y, GRID_Z
-    )
+        name="mesh",
+    )(gathered, *turn_x, *turn_y, column, row, deep, table)
+    parts = lax.all_to_all(
+        partial.reshape(devices, 3 * atom_total // 128, 128),
+        ("gx", "gy"),
+        split_axis=0,
+        concat_axis=0,
+        tiled=True,
+    )
+    total = jnp.sum(parts, axis=0).reshape(3, atom_total)
+    return total * (-own_charge / spacing)
 
 
 def convolved_by_lines(charge_mesh, count_x, count_y):
@@ -313,6 +427,64 @@
     return exchange(lines, "gx", split_axis=0, concat_axis=2)
 
 
+def far_by_lines(atoms, base, count_x, count_y, cells_x, cells_y, cells_z):
+    atom_total = atoms.shape[1]
+    cells = (cells_x, cells_y, cells_z)
+    pad = (round_up(cells_x + 3, rows_group), round_up(cells_y + 3, 8))
+    pad_x, pad_y = pad
+    turn_z = jnp.asarray(hartley(GRID_Z))
+    spread = pl.pallas_call(
+        functools.partial(spread_kernel, cells, pad),
+        out_shape=jax.ShapeDtypeStruct((pad_x, pad_y, GRID_Z), jnp.float32),
+        scratch_shapes=[
+            pltpu.VMEM((pad_x, atom_total), jnp.float32),
+            pltpu.VMEM((pad_y, atom_total), jnp.float32),
+            pltpu.VMEM((atom_total, 2 * GRID_Z), jnp.bfloat16),
+            pltpu.VMEM((rows_group * pad_y, atom_total), jnp.bfloat16),
+            pltpu.VMEM((rows_group * pad_y, atom_total), jnp.bfloat16),
+        ],
+        name="spread",
+    )(atoms, base, turn_z)
+
+    from_x = moved(spread[cells_x : cells_x + 3, :cells_y], 1, 0)
+    from_y = moved(spread[:cells_x, cells_y : cells_y + 3], 0, 1)
+    from_both = moved(spread[cells_x : cells_x + 3, cells_y : cells_y + 3], 1, 1)
+    charge_mesh = (
+        spread[:cells_x, :cells_y]
+        .at[:3]
+        .add(from_x)
+        .at[:, :3]
+        .add(from_y)
+        .at[:3, :3]
+        .add(from_both)
+    )
+    potential = convolved_by_lines(charge_mesh, count_x, count_y)
+    upper_x = moved(potential[:3], -1, 0)
+    upper_y = moved(potential[:, :3], 0, -1)
+    upper_both = moved(potential[:3, :3], -1, -1)
+    wider = jnp.concatenate(
+        [
+            jnp.concatenate([potential, upper_x], axis=0),
+            jnp.concatenate([upper_y, upper_both], axis=0),
+        ],
+        axis=1,
+    )
+    wider = jnp.pad(wider, ((0, pad_x - cells_x - 3), (0, pad_y - cells_y - 3), (0, 0)))
+    return pl.pallas_call(
+        functools.partial(gather_kernel, cells, pad),
+        out_shape=jax.ShapeDtypeStruct((3, atom_total), jnp.float32),
+        scratch_shapes=[
+            pltpu.VMEM((pad_x, atom_total), jnp.float32),
+            pltpu.VMEM((pad_x, atom_total), jnp.float32),
+            pltpu.VMEM((pad_y, atom_total), jnp.float32),
+            pltpu.VMEM((pad_y, atom_total), jnp.float32),
+            pltpu.VMEM((2 * GRID_Z, 2 * atom_total), jnp.bfloat16),
+            pltpu.VMEM((rows_group * pad_y, 2 * atom_total), jnp.float32),
+        ],
+        name="gather",
+    )(atoms, base, turn_z, wider)
+
+
 def local(positions, charges, pair_lists, slab_dest, atom_counts):
     count_x = lax.axis_size("gx")
     count_y = lax.axis_size("gy")
@@ -333,80 +505,41 @@
     base = jnp.broadcast_to(
         (slab_dest[0, 0] * cells_z)[:, None], (blocks, block_size)
     ).reshape(1, atom_total)
-    cells = (cells_x, cells_y, cells_z)
-    pad = (round_up(cells_x + 3, rows_group), round_up(cells_y + 3, 8))
-    pad_x, pad_y = pad
-    turn_z = jnp.asarray(hartley(GRID_Z))
-    spread = pl.pallas_call(
-        functools.partial(spread_kernel, cells, pad),
-        out_shape=jax.ShapeDtypeStruct((pad_x, pad_y, GRID_Z), jnp.float32),
-        scratch_shapes=[
-            pltpu.VMEM((pad_x, atom_total), jnp.float32),
-            pltpu.VMEM((pad_y, atom_total), jnp.float32),
-            pltpu.VMEM((atom_total, 2 * GRID_Z), jnp.bfloat16),
-            pltpu.VMEM((rows_group * pad_y, atom_total), jnp.bfloat16),
-            pltpu.VMEM((rows_group * pad_y, atom_total), jnp.bfloat16),
-        ],
-        name="spread",
-    )(atoms, base, turn_z)
-
-    from_x = moved(spread[cells_x : cells_x + 3, :cells_y], 1, 0)
-    from_y = moved(spread[:cells_x, cells_y : cells_y + 3], 0, 1)
-    from_both = moved(spread[cells_x : cells_x + 3, cells_y : cells_y + 3], 1, 1)
-    charge_mesh = (
-        spread[:cells_x, :cells_y]
-        .at[:3]
-        .add(from_x)
-        .at[:, :3]
-        .add(from_y)
-        .at[:3, :3]
-        .add(from_both)
-    )
-    by_planes = GRID_Z % devices == 0
-    convolved = convolved_by_planes if by_planes else convolved_by_lines
-    potential = convolved(charge_mesh, count_x, count_y)
-    upper_x = moved(potential[:3], -1, 0)
-    upper_y = moved(potential[:, :3], 0, -1)
-    upper_both = moved(potential[:3, :3], -1, -1)
-    wider = jnp.concatenate(
-        [
-            jnp.concatenate([potential, upper_x], axis=0),
-            jnp.concatenate([upper_y, upper_both], axis=0),
-        ],
-        axis=1,
-    )
-    wider = jnp.pad(wider, ((0, pad_x - cells_x - 3), (0, pad_y - cells_y - 3), (0, 0)))
-    far_part = pl.pallas_call(
-        functools.partial(gather_kernel, cells, pad),
-        out_shape=jax.ShapeDtypeStruct((3, atom_total), jnp.float32),
-        scratch_shapes=[
-            pltpu.VMEM((pad_x, atom_total), jnp.float32),
-            pltpu.VMEM((pad_x, atom_total), jnp.float32),
-            pltpu.VMEM((pad_y, atom_total), jnp.float32),
-            pltpu.VMEM((pad_y, atom_total), jnp.float32),
-            pltpu.VMEM((2 * GRID_Z, 2 * atom_total), jnp.bfloat16),
-            pltpu.VMEM((rows_group * pad_y, 2 * atom_total), jnp.float32),
-        ],
-        name="gather",
-    )(atoms, base, turn_z, wider)
-
-    nearby = with_halo(packed, (("gx", 1), ("gy", 2)), 1)
-    steps_x = (jnp.arange(3, dtype=jnp.float32) - 1.0) * cells_x
-    steps_y = (jnp.arange(3, dtype=jnp.float32) - 1.0) * cells_y
-    zero_grid = jnp.zeros((3, 3), jnp.float32)
-    cell_shift = jnp.stack(
-        [steps_x[:, None] + zero_grid, steps_y[None, :] + zero_grid, zero_grid, zero_grid]
-    )
-    beside_all = (nearby + cell_shift[:, :, :, None]).reshape(4, 9 * clusters, cluster_size)
+    height, fraction = split_cells(
+        atoms[2], base[0].astype(jnp.float32), cells_z
+    )
+    height = (base[0] + height).astype(jnp.float32)
+    sent = jnp.stack([*atoms, height, fraction, fraction, fraction])
+    gathered = lax.all_gather(sent, ("gx", "gy"), axis=0, tiled=False)
+    by_planes = GRID_Z % devices == 0 and cells_y == 64 and cells_x % 8 == 0
+    if by_planes:
+        far_part = far_by_planes(gathered, charge, count_x, count_y, cells_x, cells_y)
+    else:
+        far_part = far_by_lines(atoms, base, count_x, count_y, cells_x, cells_y, cells_z)
+
     chosen = pair_lists[0, 0]
-    pick = (chosen[:, :, None] == jnp.arange(9 * clusters, dtype=jnp.int32)).astype(jnp.float32)
+    beside = chosen // clusters
+    step_x, step_y = (beside // 3 - 1, beside % 3 - 1)
+    at_x = (lax.axis_index("gx") + step_x + count_x) % count_x
+    at_y = (lax.axis_index("gy") + step_y + count_y) % count_y
+    number = (at_x * count_y + at_y) * clusters + chosen % clusters
+    pick = (number[:, :, None] == jnp.arange(devices * clusters, dtype=jnp.int32)).astype(
+        jnp.float32
+    )
+    pool = gathered[:, :4].reshape(devices, 4, clusters, cluster_size)
+    pool = jnp.transpose(pool, (1, 0, 2, 3)).reshape(4, devices * clusters, cluster_size)
     partners = jnp.einsum(
         "cln,fnk->cflk",
         pick,
-        beside_all,
+        pool,
         precision=lax.Precision.HIGHEST,
         preferred_element_type=jnp.float32,
-    ).reshape(clusters, 4, -1)
+    )
+    shift_x = (step_x * cells_x).astype(jnp.float32)
+    shift_y = (step_y * cells_y).astype(jnp.float32)
+    flat = jnp.zeros_like(shift_x)
+    shift = jnp.stack([shift_x, shift_y, flat, flat], axis=1)
+    partners = (partners + shift[:, :, :, None]).reshape(clusters, 4, -1)
     own = packed.reshape(4, clusters, cluster_size)
     pair_part = jnp.stack(
         [one_cluster(own[:, c], partners[c]) for c in range(clusters)], axis=1

time: 215 us -> 116 us (0.54)
  waiting for transfers between devices: 62.8 us -> 0.01 us
  local copies, waits for them, and re-layouts: 47.5 us -> 5.71 us
  starting transfers between devices: 36.4 us -> 3.7 us
  blocking collectives: 0 us -> 26 us
  Pallas kernels: 40.3 us -> 55.9 us
  other arithmetic: 24.6 us -> 22 us
    all_to_all x2 -> x1, waiting for transfers between devices: 49.7 us -> 0.01 us  [far_by_planes(): lax.all_to_all(partial.reshape(devices, 3 * atom_total // 128, 128), ('gx...]
    all_gather x0 -> x1, blocking collectives: none -> 26 us  [local(): gathered = lax.all_gather(sent, ('gx', 'gy'), axis=0, tiled=False)]
    reshape x6 -> x3, local copies, waits for them, and re-layouts: 24.7 us -> 2 us  [the longest x1 1.73 us: far_by_planes(): partial.reshape(devices, 3 * atom_total // 128, 128)]
    ppermute x10 -> x0, starting transfers between devices: 20.2 us -> none  [the longest x6 13.4 us: moved(): return lax.ppermute(value, ('gx', 'gy'), pairs)]
    pallas_call x3 -> x1, Pallas kernels: 40.3 us -> 55.9 us  [far_by_planes(): pl.pallas_call(functools.partial(mesh_kernel, (count_x, count_y), (cells_...]
    ppermute x10 -> x0, waiting for transfers between devices: 13.2 us -> none  [the longest x2 6.56 us: with_halo(): after = lax.ppermute(initial, axis, down)]
    all_to_all x2 -> x1, starting transfers between devices: 16.1 us -> 3.7 us  [far_by_planes(): lax.all_to_all(partial.reshape(devices, 3 * atom_total // 128, 128), ('gx...]
    transpose x3 -> x2, local copies, waits for them, and re-layouts: 10.4 us -> 0.81 us  [the longest x1 0.79 us: far_by_planes(): column = green_factors(jnp.arange(GRID_X, dtype=jnp.int32), GRID_X).T]
  transfers between devices with their start and end apart: 12 -> 1, of which waited for: 6 -> 0; matrix products, arithmetic and copies ran while one was open for 15% -> 16% of each run, Pallas kernels for 5% -> 0%
where the time goes in v2:
time: 116 us; the launch traced here: 115 us
  Pallas kernels  55.9 us (48%)
  blocking collectives  26 us (22%)
  other arithmetic  22 us (19%)
  local copies, waits for them, and re-layouts  5.71 us (5%)
  starting transfers between devices  3.7 us (3%)
  between operations  1.65 us (1%)
    pallas_call x1, Pallas kernels, far_by_planes(): pl.pallas_call(functools.partial(mesh_kernel, (count_x, count_y), (cells_...  55.9 us
    all_gather x1, blocking collectives, local(): gathered = lax.all_gather(sent, ('gx', 'gy'), axis=0, tiled=False)  26 us
    mul x8, other arithmetic, one_cluster(): return own_rows[3] * jnp.sum(weight[None] * offsets, axis=2)  12.3 us
    all_to_all x1, starting transfers between devices, far_by_planes(): lax.all_to_all(partial.reshape(devices, 3 * atom_total // 128, 128), ('gx...  3.7 us
  transfers between devices with their start and end apart: 1, of which 0 were waited for; matrix products, arithmetic and copies ran while one was open for 16% of the time, Pallas kernels for 0%

profile of v2, /device:TPU:0, one launch (start us, length us, event | category | flops | bytes accessed | tf_op | source)
XLA Modules:
  0.0 115.1 jit_solution(6204657979851498895)
XLA Ops:
  1.4 0.7 multiply_bitcast_fusion
  2.1 0.7 fusion.92
  2.8 0.7 copy.21.depth_ref
  3.5 0.7 slice_bitcast_fusion.8
  4.3 0.7 add_convert_fusion.1
  5.1 0.6 pad_maximum_fusion.2
  5.7 0.8 copy.20.column_ref
  6.5 0.7 compare_select_fusion
  7.3 26.0 %all-gather = f32[128,1024]{1,0:T(8,128)} all-gather(f32[8,1024]{1,0:T(8,128)S(1)} %stack.12), channel_id=2, replica_groups=mesh['rep'=2,'gx'=4,'gy'=4] {'gx','gy'}, dimensions={0}, use_global_device_ids=true | all-gather | bytes 557056 | tf_op jit(solution)/shard_map/all_gather | solution.py:513
  33.3 0.7 pad_maximum_fusion.1.table_ref
  33.9 55.9 %mesh.1 = f32[16,3,1024]{2,1,0:T(4,128)} custom-call(f32[16,8,1024]{2,1,0:T(8,128)} %bitcast.134, bf16[256,256]{1,0:T(8,128)(2,1)} %constant.188.xh_ref.yh_ref, bf16[256,256]{1,0:T(8,128)(2,1)} %constant.191.xl_ref.yl_ref, bf16[256,256]{1,0:T(8,128)(2,1)} %constant.188.xh_ref.yh_ref, bf16[256,256]{1,0:T(8,128)(2,1)} %constant.191.xl_ref.yl_ref, ...), custom_call_target="tpu_custom_call" | custom-call | tf_op jit(solution)/shard_map/mesh/pallas_call | solution.py:373
  89.8 1.7 %reshape.1110 = f32[16,24,128]{2,1,0:T(8,128)} reshape(f32[16,3,1024]{2,1,0:T(4,128)} %mesh.1) | data formatting | bytes 393216 | tf_op jit(solution)/shard_map/reshape | solution.py:393
  91.5 3.7 %all-to-all-start = ((f32[16,24,128]{2,1,0:T(8,128)}), f32[16,24,128]{2,1,0:T(8,128)S(1)}, u32[]{:S(2)}, u32[]{:S(2)}) async-start(f32[16,24,128]{2,1,0:T(8,128)} %reshape.1110), calls=%async_computation | async-start | bytes 393216 | tf_op jit(solution)/shard_map/all_to_all | solution.py:392
  96.2 0.5 broadcast.1722
  96.7 0.7 reduce.4
  98.0 3.1 %multiply_multiply_fusion.4 = f32[256,1024]{1,0:T(8,128)S(1)} fusion(f32[256,1024]{1,0:T(8,128)S(1)} %fusion.4, f32[1024]{0:T(1024)S(1)} %bitcast.153), kind=kLoop, calls=%fused_computation.74 | loop fusion | flops 19922944 | bytes 2101248 | tf_op jit(solution)/shard_map/mul | solution.py:346
  101.1 0.5 fusion.5
  102.1 3.1 %multiply_multiply_fusion.2 = f32[256,1024]{1,0:T(8,128)S(1)} fusion(f32[256,1024]{1,0:T(8,128)S(1)} %fusion.7, f32[1024]{0:T(1024)S(1)} %bitcast.152), kind=kLoop, calls=%fused_computation.64 | loop fusion | flops 19922944 | bytes 2101248 | tf_op jit(solution)/shard_map/mul | solution.py:346
  105.2 0.5 fusion.8
  106.2 3.1 %multiply_multiply_fusion = f32[256,1024]{1,0:T(8,128)S(1)} fusion(f32[256,1024]{1,0:T(8,128)S(1)} %fusion.10, f32[1024]{0:T(1024)S(1)} %bitcast.151), kind=kLoop, calls=%fused_computation.54 | loop fusion | flops 19922944 | bytes 2101248 | tf_op jit(solution)/shard_map/mul | solution.py:346
  109.2 0.5 fusion.11
  110.2 3.1 %multiply_multiply_fusion.6 = f32[256,1024]{1,0:T(8,128)S(1)} fusion(f32[256,1024]{1,0:T(8,128)S(1)} %fusion.1, f32[1024]{0:T(1024)S(1)} %bitcast.150), kind=kLoop, calls=%fused_computation.84 | loop fusion | flops 19922944 | bytes 2101248 | tf_op jit(solution)/shard_map/mul | solution.py:346
  113.9 0.6 copy.22
  114.5 0.6 broadcast_multiply_fusion
  (56 shorter events, 3.7 us)
Async XLA Ops:
  33.9 61.3 %copy-start.3 = (s32[1,1,4,4]{3,2,1,0:T(4,128)S(1)}, s32[1,1,4,4]{3,2,1,0:T(4,128)}, u32[]{:S(2)}) copy-start(s32[1,1,4,4]{3,2,1,0:T(4,128)} %param.10) | copy-start | bytes 196
  33.9 61.4 %copy-start = (f32[128,1024]{1,0:T(8,128)S(1)}, f32[128,1024]{1,0:T(8,128)}, u32[]{:S(2)}) copy-start(f32[128,1024]{1,0:T(8,128)} %all-gather) | copy-start | bytes 1572868
  91.5 22.9 %all-to-all-start = ((f32[16,24,128]{2,1,0:T(8,128)}), f32[16,24,128]{2,1,0:T(8,128)S(1)}, u32[]{:S(2)}, u32[]{:S(2)}) async-start(f32[16,24,128]{2,1,0:T(8,128)} %reshape.1110), calls=%async_computation | async-start | bytes 393216 | tf_op jit(solution)/shard_map/all_to_all | solution.py:392
  95.4 0.8 copy-start.1
  95.4 1.3 %copy-start.2 = (f32[1,1,1024]{2,1,0:T(1,128)S(1)}, f32[1,1,1024]{2,1,0:T(1,128)}, u32[]{:S(2)}) copy-start(f32[1,1,1024]{2,1,0:T(1,128)} %param.9) | copy-start | bytes 12292

commit v3 on v2

--- a/solution.py
+++ b/solution.py
@@ -177,6 +177,54 @@
         out_ref[pl.ds(place, 1), :] = factor * jnp.sum(sums[place], axis=0, keepdims=True)
 
 
+def share_kernel(sizes, atoms_ref, out_ref, send_sem, recv_sem):
+    count_x, count_y = sizes
+    place_x, place_y = (lax.axis_index("gx"), lax.axis_index("gy"))
+    me = place_x * count_y + place_y
+    peers = []
+    for order in range(1, count_x * count_y):
+        peer_x = lax.rem(place_x + order // count_y, count_x)
+        peer_y = lax.rem(place_y + order % count_y, count_y)
+        peers.append({"gx": peer_x, "gy": peer_y})
+    barrier = pltpu.get_barrier_semaphore()
+    for peer in peers:
+        pl.semaphore_signal(
+            barrier, inc=1, device_id=peer, device_id_type=pl.DeviceIdType.MESH
+        )
+    pl.semaphore_wait(barrier, len(peers))
+    copies = [
+        pltpu.make_async_remote_copy(
+            src_ref=atoms_ref,
+            dst_ref=out_ref.at[me],
+            send_sem=send_sem.at[order],
+            recv_sem=recv_sem.at[order],
+            device_id=peer,
+            device_id_type=pl.DeviceIdType.MESH,
+        )
+        for order, peer in enumerate(peers)
+    ]
+    for copy in copies:
+        copy.start()
+    out_ref[me] = atoms_ref[...]
+    for copy in copies:
+        copy.wait()
+
+
+def shared(atoms, count_x, count_y):
+    devices = count_x * count_y
+    vmem = pl.BlockSpec(memory_space=pltpu.VMEM)
+    flags = pltpu.SemaphoreType.DMA((devices - 1,))
+    return pl.pallas_call(
+        functools.partial(share_kernel, (count_x, count_y)),
+        in_specs=[vmem],
+        out_specs=vmem,
+        out_shape=jax.ShapeDtypeStruct((devices, *atoms.shape), jnp.float32),
+        scratch_shapes=[flags, flags],
+        compiler_params=pltpu.CompilerParams(collective_id=0, has_side_effects=True),
+        name="share",
+    )(atoms)
+
+
 def depth_rows(table, height, fraction, terms):
     turns = (height * table[:, 0:1]).astype(jnp.int32) % GRID_Z
     phases = turns.astype(jnp.float32) * (2.0 * math.pi / GRID_Z)
@@ -189,31 +237,37 @@
     return results
 
 
-def mesh_kernel(sizes, cells, pad, atoms_ref, xh_ref, xl_ref, yh_ref, yl_ref, column_ref, row_ref, depth_ref, table_ref, out_ref, wx_ref, vx_ref, wy_ref, hi_ref, lo_ref, mesh_ref, turned_ref, level_ref, stack_ref, side_ref):
+def mesh_kernel(sizes, cells, pad, atoms_ref, xh_ref, xl_ref, yh_ref, yl_ref, column_ref, row_ref, table_ref, out_ref, mesh_ref, turned_ref, *scratch):
     count_x, count_y = sizes
     cells_x, cells_y = cells
     pad_x, pad_y = pad
     atom_total = atoms_ref.shape[2]
-    depth = depth_ref.shape[0]
+    depth = table_ref.shape[0]
     window = 2 * cells_y
     windows = GRID_Y // window
     lane = lax.broadcasted_iota(jnp.int32, (depth * pad_x, window), 1)
     mesh_ref[...] = jnp.zeros_like(mesh_ref)
-    wy_ref[...] = jnp.zeros_like(wy_ref)
     table = table_ref[...]
+    per_side = len(scratch) // 2
+    banks = (scratch[:per_side], scratch[per_side:])
+    for _, _, wy_ref, _, _, _, _, side_ref in banks:
+        wy_ref[...] = jnp.zeros_like(wy_ref)
+        side_ref[...] = jnp.zeros_like(side_ref)
 
     def atoms_of(cell, row):
         return atoms_ref[cell, row : row + 1, :]
 
     def spread_cell(cell, i, j):
+        wx_ref, vx_ref, wy_ref, hi_ref, lo_ref, level_ref, stack_ref, side_ref = banks[j % 2]
         low_x, frac_x = split_cells(atoms_of(cell, 0), 0.0, cells_x)
         low_y, frac_y = split_cells(atoms_of(cell, 1), 0.0, cells_y)
         wx_ref[...] = spline_table(low_x, spline_weights(frac_x)[0], pad_x)
         high, low = halves(spline_table(low_y, spline_weights(frac_y)[0], pad_y))
         wy_ref[:pad_y, :] = high
         wy_ref[pl.ds(window, pad_y), :] = low
-        frac_z = atoms_of(cell, 5)
-        (deep,) = depth_rows(table, atoms_of(cell, 4), frac_z, [spline_weights(frac_z)[0]])
+        height = jnp.floor(atoms_of(cell, 2))
+        frac_z = atoms_of(cell, 2) - height
+        (deep,) = depth_rows(table, height, frac_z, [spline_weights(frac_z)[0]])
         deep = deep * atoms_of(cell, 3)
         for k in range(depth):
             high, low = halves(deep[k : k + 1, :] * wx_ref[...])
@@ -260,8 +314,8 @@
     def _(k):
         mesh_ref[k, :extra, :] += mesh_ref[k, GRID_X:, :]
         waves = along(across(mesh_ref[k, :GRID_X, :]))
-        square = column_ref[:, 0:1] + row_ref[0:1, :] + depth_ref[k, 0:1, 0:1]
-        scale = column_ref[:, 1:2] * row_ref[1:2, :] * depth_ref[k, 0:1, 1:2]
+        square = column_ref[:, 0:1] + row_ref[0:1, :] + table_ref[pl.ds(k, 1), 9:10]
+        scale = column_ref[:, 1:2] * row_ref[1:2, :] * table_ref[pl.ds(k, 1), 10:11]
         green = jnp.where(square > 0.0, scale / jnp.where(square > 0.0, square, 1.0), 0.0)
         plane = across(along(waves * green))
         mesh_ref[k, :GRID_X, :] = plane
@@ -271,10 +325,10 @@
         turned_ref[k, GRID_X:, :] = rolled[:extra]
 
     stride = round_up(pad_y, 16)
-    side_ref[...] = jnp.zeros_like(side_ref)
     groups = pad_x // 8
 
     def gather_cell(cell, i, j):
+        wx_ref, vx_ref, wy_ref, hi_ref, lo_ref, level_ref, stack_ref, side_ref = banks[j % 2]
         low_x, frac_x = split_cells(atoms_of(cell, 0), 0.0, cells_x)
         low_y, frac_y = split_cells(atoms_of(cell, 1), 0.0, cells_y)
         values, slopes = spline_weights(frac_x)
@@ -286,8 +340,9 @@
             side_ref[:stride, span] = high
             side_ref[pl.ds(stride, stride), span] = low
             side_ref[pl.ds(2 * stride, stride), span] = high
-        frac_z = atoms_of(cell, 5)
-        deep, steep = depth_rows(table, atoms_of(cell, 4), frac_z, spline_weights(frac_z))
+        height = jnp.floor(atoms_of(cell, 2))
+        frac_z = atoms_of(cell, 2) - height
+        deep, steep = depth_rows(table, height, frac_z, spline_weights(frac_z))
         source = mesh_ref if j % 2 == 0 else turned_ref
         rows = pl.ds(pl.multiple_of(i * cells_x, 8), pad_x)
         block = source[:, rows, pl.ds(j // 2 * window, window)].reshape(depth * pad_x, window)
@@ -313,11 +368,22 @@
             third = third + steep[k : k + 1, :] * part_z
         for place, value in enumerate((first, second, third)):
             out_ref[cell, pl.ds(place, 1), :] = jnp.sum(value, axis=0, keepdims=True)
+        out_ref[cell, 3:4, :] = jnp.zeros((1, atom_total), jnp.float32)
 
     @pl.loop(0, count_x)
     def _(i):
         for j in range(count_y):
             gather_cell(i * count_y + j, i, j)
+
+
+def green_table(period):
+    index = np.arange(period)
+    signed = np.where(index <= period // 2, index, index - period) / (period * spacing)
+    modulus = ((2.0 + np.cos(index * (2.0 * np.pi / period))) / 3.0) ** 2
+    square = signed * signed
+    return np.stack([square, np.exp(-((np.pi / ewald_split) ** 2) * square) / modulus]).astype(
+        np.float32
+    )
 
 
 def green_factors(index, period):
@@ -357,46 +423,44 @@
     turn_x = halves(jnp.asarray(hartley(GRID_X)))
     turn_y = halves(jnp.asarray(hartley(GRID_Y)))
     volume = GRID_X * GRID_Y * GRID_Z * spacing**3
-    column = green_factors(jnp.arange(GRID_X, dtype=jnp.int32), GRID_X).T
-    row = green_factors(jnp.arange(GRID_Y, dtype=jnp.int32), GRID_Y)
-    own_k = place * depth + jnp.arange(depth, dtype=jnp.int32)
-    deep = green_factors(own_k, GRID_Z)
-    deep = (deep * jnp.array([[1.0], [1.0 / (math.pi * volume)]], jnp.float32)).T[:, None, :]
-    taps = (own_k[:, None] * jnp.arange(4, dtype=jnp.int32)).astype(jnp.float32)
-    taps = taps * (2.0 * math.pi / GRID_Z)
-    cosine, sine = (jnp.cos(taps), jnp.sin(taps))
-    table = jnp.concatenate(
-        [own_k[:, None].astype(jnp.float32), cosine + sine, cosine - sine], axis=1
-    )
+    column = jnp.asarray(green_table(GRID_X).T)
+    row = jnp.asarray(green_table(GRID_Y))
+    every_k = np.arange(GRID_Z)
+    taps = np.outer(every_k, np.arange(4)) * (2.0 * np.pi / GRID_Z)
+    square, scale = green_table(GRID_Z)
+    table = np.concatenate(
+        [
+            every_k[:, None],
+            np.cos(taps) + np.sin(taps),
+            np.cos(taps) - np.sin(taps),
+            square[:, None],
+            scale[:, None] / (np.pi * volume),
+        ],
+        axis=1,
+    ).astype(np.float32)
+    table = lax.dynamic_slice_in_dim(jnp.asarray(table), place * depth, depth, axis=0)
     vmem = pl.BlockSpec(memory_space=pltpu.VMEM)
     rows = GRID_X + pad_x - cells_x
+    bank = [
+        pltpu.VMEM((pad_x, atom_total), jnp.float32),
+        pltpu.VMEM((pad_x, atom_total), jnp.float32),
+        pltpu.VMEM((2 * window, atom_total), jnp.bfloat16),
+        pltpu.VMEM((depth * pad_x, atom_total), jnp.bfloat16),
+        pltpu.VMEM((depth * pad_x, atom_total), jnp.bfloat16),
+        pltpu.VMEM((depth * pad_x, 2 * atom_total), jnp.float32),
+        pltpu.VMEM((depth * pad_x, 2 * window), jnp.bfloat16),
+        pltpu.VMEM((2 * window, 2 * atom_total), jnp.bfloat16),
+    ]
     partial = pl.pallas_call(
         functools.partial(mesh_kernel, (count_x, count_y), (cells_x, cells_y), (pad_x, pad_y)),
-        in_specs=[vmem] * 9,
+        in_specs=[vmem] * 8,
         out_specs=vmem,
-        out_shape=jax.ShapeDtypeStruct((devices, 3, atom_total), jnp.float32),
-        scratch_shapes=[
-            pltpu.VMEM((pad_x, atom_total), jnp.float32),
-            pltpu.VMEM((pad_x, atom_total), jnp.float32),
-            pltpu.VMEM((2 * window, atom_total), jnp.bfloat16),
-            pltpu.VMEM((depth * pad_x, atom_total), jnp.bfloat16),
-            pltpu.VMEM((depth * pad_x, atom_total), jnp.bfloat16),
-            pltpu.VMEM((depth, rows, GRID_Y), jnp.float32),
-            pltpu.VMEM((depth, rows, GRID_Y), jnp.float32),
-            pltpu.VMEM((depth * pad_x, 2 * atom_total), jnp.float32),
-            pltpu.VMEM((depth * pad_x, 2 * window), jnp.bfloat16),
-            pltpu.VMEM((2 * window, 2 * atom_total), jnp.bfloat16),
-        ],
+        out_shape=jax.ShapeDtypeStruct((devices, 4, atom_total), jnp.float32),
+        scratch_shapes=[pltpu.VMEM((depth, rows, GRID_Y), jnp.float32)] * 2 + 2 * bank,
         name="mesh",
-    )(gathered, *turn_x, *turn_y, column, row, deep, table)
-    parts = lax.all_to_all(
-        partial.reshape(devices, 3 * atom_total // 128, 128),
-        ("gx", "gy"),
-        split_axis=0,
-        concat_axis=0,
-        tiled=True,
-    )
-    total = jnp.sum(parts, axis=0).reshape(3, atom_total)
+    )(gathered, *turn_x, *turn_y, column, row, table)
+    parts = lax.all_to_all(partial, ("gx", "gy"), split_axis=0, concat_axis=0, tiled=True)
+    total = jnp.sum(parts, axis=0)[:3]
     return total * (-own_charge / spacing)
 
 
@@ -505,13 +569,11 @@
     base = jnp.broadcast_to(
         (slab_dest[0, 0] * cells_z)[:, None], (blocks, block_size)
     ).reshape(1, atom_total)
-    height, fraction = split_cells(
-        atoms[2], base[0].astype(jnp.float32), cells_z
-    )
-    height = (base[0] + height).astype(jnp.float32)
-    sent = jnp.stack([*atoms, height, fraction, fraction, fraction])
-    gathered = lax.all_gather(sent, ("gx", "gy"), axis=0, tiled=False)
     by_planes = GRID_Z % devices == 0 and cells_y == 64 and cells_x % 8 == 0
+    if by_planes:
+        gathered = shared(atoms, count_x, count_y)
+    else:
+        gathered = lax.all_gather(atoms, ("gx", "gy"), axis=0, tiled=False)
     if by_planes:
         far_part = far_by_planes(gathered, charge, count_x, count_y, cells_x, cells_y)
     else:

time: 116 us -> 99.5 us (0.86)
  blocking collectives: 26 us -> 0 us
  Pallas kernels: 55.9 us -> 68.3 us
  other arithmetic: 22 us -> 18.4 us
  starting transfers between devices: 3.7 us -> 6.12 us
  local copies, waits for them, and re-layouts: 5.71 us -> 4.27 us
    all_gather x1 -> x0, blocking collectives: 26 us -> none  [local(): gathered = lax.all_gather(sent, ('gx', 'gy'), axis=0, tiled=False)]
    pallas_call x0 -> x1, Pallas kernels: none -> 13.4 us  [shared(): pl.pallas_call(functools.partial(share_kernel, (count_x, count_y)), in_sp...]
    all_to_all x1, starting transfers between devices: 3.7 us -> 6.12 us  [far_by_planes(): lax.all_to_all(partial, ('gx', 'gy'), split_axis=0, concat_axis=0, tiled=...]
    dynamic_slice x0 -> x1, local copies, waits for them, and re-layouts: none -> 1.33 us  [far_by_planes(): lax.dynamic_slice_in_dim(jnp.asarray(table), place * depth, depth, axis=0)]
  transfers between devices with their start and end apart: 1 -> 1, of which waited for: 0 -> 0; matrix products, arithmetic and copies ran while one was open for 16% -> 19% of each run, Pallas kernels for 0% -> 0%
where the time goes in v3:
time: 99.5 us; the launch traced here: 99 us
  Pallas kernels  68.3 us (69%)
  other arithmetic  18.4 us (18%)
  starting transfers between devices  6.12 us (6%)
  local copies, waits for them, and re-layouts  4.27 us (4%)
  between operations  1.64 us (2%)
    pallas_call x1, Pallas kernels, far_by_planes(): pl.pallas_call(functools.partial(mesh_kernel, (count_x, count_y), (cells_...  54.9 us
    pallas_call x1, Pallas kernels, shared(): pl.pallas_call(functools.partial(share_kernel, (count_x, count_y)), in_sp...  13.4 us
    mul x8, other arithmetic, one_cluster(): return own_rows[3] * jnp.sum(weight[None] * offsets, axis=2)  12.3 us
    all_to_all x1, starting transfers between devices, far_by_planes(): lax.all_to_all(partial, ('gx', 'gy'), split_axis=0, concat_axis=0, tiled=...  6.12 us
    reduce_sum x4, other arithmetic, one_cluster(): return own_rows[3] * jnp.sum(weight[None] * offsets, axis=2)  2.04 us
  transfers between devices with their start and end apart: 1, of which 0 were waited for; matrix products, arithmetic and copies ran while one was open for 19% of the time, Pallas kernels for 0%

profile of v3, /device:TPU:0, one launch (start us, length us, event | category | flops | bytes accessed | tf_op | source)
XLA Modules:
  0.0 99.0 jit_solution(7615027012542535041)
XLA Ops:
  1.3 0.7 copy.15
  2.0 0.7 compare_select_fusion
  2.7 0.6 maximum_bitcast_fusion.atoms_ref
  3.3 13.4 %share.1.atoms_ref = f32[16,4,1024]{2,1,0:T(4,128)} custom-call(f32[4,1024]{1,0:T(4,128)} %maximum_bitcast_fusion.atoms_ref), custom_call_target="tpu_custom_call" | custom-call | tf_op jit(solution)/shard_map/share/pallas_call | solution.py:217
  16.7 1.3 %constant_dynamic-slice_fusion.table_ref = f32[8,11]{1,0:T(8,128)} fusion(f32[128,11]{1,0:T(8,128)} %constant.156.clone, s32[]{:T(128)S(6)} %select_n.155), kind=kLoop, calls=%fused_computation.169 | loop fusion | bytes 708 | tf_op jit(solution)/shard_map/dynamic_slice | solution.py:441
  18.0 54.9 %mesh.1 = f32[16,4,1024]{2,1,0:T(4,128)} custom-call(f32[16,4,1024]{2,1,0:T(4,128)} %share.1.atoms_ref, bf16[256,256]{1,0:T(8,128)(2,1)} %constant.161.xh_ref.yh_ref, bf16[256,256]{1,0:T(8,128)(2,1)} %constant.164.xl_ref.yl_ref, bf16[256,256]{1,0:T(8,128)(2,1)} %constant.161.xh_ref.yh_ref, bf16[256,256]{1,0:T(8,128)(2,1)} %constant.164.xl_ref.yl_ref, ...), custom_call_target="tpu_custom_call" | custom-call | tf_op jit(solution)/shard_map/mesh/pallas_call | solution.py:454
  73.0 6.1 %all-to-all-start = ((f32[16,4,1024]{2,1,0:T(4,128)}), f32[16,4,1024]{2,1,0:T(4,128)S(1)}, u32[]{:S(2)}, u32[]{:S(2)}) async-start(f32[16,4,1024]{2,1,0:T(4,128)} %mesh.1), calls=%async_computation | async-start | bytes 524288 | tf_op jit(solution)/shard_map/all_to_all | solution.py:462
  79.7 0.3 fusion.12
  80.0 0.5 broadcast.1440
  80.5 0.7 reduce.4
  81.4 0.4 fusion.4
  81.9 3.1 %multiply_multiply_fusion.4 = f32[256,1024]{1,0:T(8,128)S(1)} fusion(f32[256,1024]{1,0:T(8,128)S(1)} %fusion.4, f32[1024]{0:T(1024)S(1)} %bitcast.129), kind=kLoop, calls=%fused_computation.74 | loop fusion | flops 19922944 | bytes 2101248 | tf_op jit(solution)/shard_map/mul | solution.py:412
  84.9 0.5 fusion.5
  85.5 0.4 fusion.7
  85.9 3.1 %multiply_multiply_fusion.2 = f32[256,1024]{1,0:T(8,128)S(1)} fusion(f32[256,1024]{1,0:T(8,128)S(1)} %fusion.7, f32[1024]{0:T(1024)S(1)} %bitcast.128), kind=kLoop, calls=%fused_computation.64 | loop fusion | flops 19922944 | bytes 2101248 | tf_op jit(solution)/shard_map/mul | solution.py:412
  89.0 0.5 fusion.8
  89.5 0.4 fusion.10
  90.0 3.1 %multiply_multiply_fusion = f32[256,1024]{1,0:T(8,128)S(1)} fusion(f32[256,1024]{1,0:T(8,128)S(1)} %fusion.10, f32[1024]{0:T(1024)S(1)} %bitcast.127), kind=kLoop, calls=%fused_computation.54 | loop fusion | flops 19922944 | bytes 2101248 | tf_op jit(solution)/shard_map/mul | solution.py:412
  93.1 0.5 fusion.11
  93.6 0.4 fusion.1
  94.0 3.1 %multiply_multiply_fusion.6 = f32[256,1024]{1,0:T(8,128)S(1)} fusion(f32[256,1024]{1,0:T(8,128)S(1)} %fusion.1, f32[1024]{0:T(1024)S(1)} %bitcast.126), kind=kLoop, calls=%fused_computation.84 | loop fusion | flops 19922944 | bytes 2101248 | tf_op jit(solution)/shard_map/mul | solution.py:412
  97.1 0.5 fusion.2
  97.7 0.6 copy.17
  98.4 0.6 reshape.887
  (43 shorter events, 0.8 us)
Async XLA Ops:
  0.6 78.5 %copy-start.3 = (s32[1,1,4,4]{3,2,1,0:T(4,128)S(1)}, s32[1,1,4,4]{3,2,1,0:T(4,128)}, u32[]{:S(2)}) copy-start(s32[1,1,4,4]{3,2,1,0:T(4,128)} %param.12) | copy-start | bytes 196
  16.7 62.5 %copy-start = (f32[16,4,1024]{2,1,0:T(4,128)S(1)}, f32[16,4,1024]{2,1,0:T(4,128)}, u32[]{:S(2)}) copy-start(f32[16,4,1024]{2,1,0:T(4,128)} %share.1.atoms_ref) | copy-start | bytes 786436
  73.0 25.3 %all-to-all-start = ((f32[16,4,1024]{2,1,0:T(4,128)}), f32[16,4,1024]{2,1,0:T(4,128)S(1)}, u32[]{:S(2)}, u32[]{:S(2)}) async-start(f32[16,4,1024]{2,1,0:T(4,128)} %mesh.1), calls=%async_computation | async-start | bytes 524288 | tf_op jit(solution)/shard_map/all_to_all | solution.py:462
  79.1 0.9 copy-start.1
  79.2 1.3 %copy-start.2 = (f32[1,1,1024]{2,1,0:T(1,128)S(1)}, f32[1,1,1024]{2,1,0:T(1,128)}, u32[]{:S(2)}) copy-start(f32[1,1,1024]{2,1,0:T(1,128)} %param.11) | copy-start | bytes 12292

commit v4 on v3

--- a/solution.py
+++ b/solution.py
@@ -226,9 +226,25 @@
 
 
 def depth_rows(table, height, fraction, terms):
-    turns = (height * table[:, 0:1]).astype(jnp.int32) % GRID_Z
-    phases = turns.astype(jnp.float32) * (2.0 * math.pi / GRID_Z)
-    cosine, sine = (jnp.cos(phases), jnp.sin(phases))
+    turns = height * table[:, 0:1]
+    quarter = GRID_Z // 4
+    nearest = jnp.floor(turns * (1.0 / quarter) + 0.5)
+    angle = (turns - nearest * quarter) * (2.0 * math.pi / GRID_Z)
+    quadrant = nearest - 4.0 * jnp.floor(nearest * 0.25)
+    square = angle * angle
+    near_cos = 1.0 + square * (
+        -0.5 + square * (1.0 / 24.0 + square * (-1.0 / 720.0 + square * (1.0 / 40320.0)))
+    )
+    near_sin = angle * (
+        1.0
+        + square
+        * (-1.0 / 6.0 + square * (1.0 / 120.0 + square * (-1.0 / 5040.0 + square / 362880.0)))
+    )
+    odd_turn = (quadrant == 1.0) | (quadrant == 3.0)
+    cosine = jnp.where(odd_turn, near_sin, near_cos)
+    cosine = jnp.where((quadrant == 1.0) | (quadrant == 2.0), -cosine, cosine)
+    sine = jnp.where(odd_turn, near_cos, near_sin)
+    sine = jnp.where(quadrant >= 2.0, -sine, sine)
     results = []
     for weights in terms:
         even = sum(table[:, 1 + t : 2 + t] * weights[t] for t in range(4))

time: 99.5 us -> 96.7 us (0.972)
  Pallas kernels: 68.3 us -> 65.6 us
    pallas_call x1, Pallas kernels: 54.9 us -> 52.3 us  [far_by_planes(): pl.pallas_call(functools.partial(mesh_kernel, (count_x, count_y), (cells_...]
  transfers between devices with their start and end apart: 1 -> 1, of which waited for: 0 -> 0; matrix products, arithmetic and copies ran while one was open for 19% -> 20% of each run, Pallas kernels for 0% -> 0%
where the time goes in v4:
time: 96.7 us; the launch traced here: 96.2 us
  Pallas kernels  65.6 us (68%)
  other arithmetic  18.4 us (19%)
  starting transfers between devices  5.97 us (6%)
  local copies, waits for them, and re-layouts  4.27 us (4%)
  between operations  1.64 us (2%)
    pallas_call x1, Pallas kernels, far_by_planes(): pl.pallas_call(functools.partial(mesh_kernel, (count_x, count_y), (cells_...  52.3 us
    pallas_call x1, Pallas kernels, shared(): pl.pallas_call(functools.partial(share_kernel, (count_x, count_y)), in_sp...  13.4 us
    mul x8, other arithmetic, one_cluster(): return own_rows[3] * jnp.sum(weight[None] * offsets, axis=2)  12.3 us
    all_to_all x1, starting transfers between devices, far_by_planes(): lax.all_to_all(partial, ('gx', 'gy'), split_axis=0, concat_axis=0, tiled=...  5.97 us
    reduce_sum x4, other arithmetic, one_cluster(): return own_rows[3] * jnp.sum(weight[None] * offsets, axis=2)  2.04 us
  transfers between devices with their start and end apart: 1, of which 0 were waited for; matrix products, arithmetic and copies ran while one was open for 20% of the time, Pallas kernels for 0%

profile of v4, /device:TPU:0, one launch (start us, length us, event | category | flops | bytes accessed | tf_op | source)
XLA Modules:
  0.0 96.2 jit_solution(10155256270435562340)
XLA Ops:
  1.3 0.7 copy.15
  2.0 0.7 compare_select_fusion
  2.7 0.6 maximum_bitcast_fusion.atoms_ref
  3.3 13.4 %share.1.atoms_ref = f32[16,4,1024]{2,1,0:T(4,128)} custom-call(f32[4,1024]{1,0:T(4,128)} %maximum_bitcast_fusion.atoms_ref), custom_call_target="tpu_custom_call" | custom-call | tf_op jit(solution)/shard_map/share/pallas_call | solution.py:217
  16.7 1.3 %constant_dynamic-slice_fusion.table_ref = f32[8,11]{1,0:T(8,128)} fusion(f32[128,11]{1,0:T(8,128)} %constant.156.clone, s32[]{:T(128)S(6)} %select_n.155), kind=kLoop, calls=%fused_computation.169 | loop fusion | bytes 708 | tf_op jit(solution)/shard_map/dynamic_slice | solution.py:457
  18.0 52.3 %mesh.1 = f32[16,4,1024]{2,1,0:T(4,128)} custom-call(f32[16,4,1024]{2,1,0:T(4,128)} %share.1.atoms_ref, bf16[256,256]{1,0:T(8,128)(2,1)} %constant.161.xh_ref.yh_ref, bf16[256,256]{1,0:T(8,128)(2,1)} %constant.164.xl_ref.yl_ref, bf16[256,256]{1,0:T(8,128)(2,1)} %constant.161.xh_ref.yh_ref, bf16[256,256]{1,0:T(8,128)(2,1)} %constant.164.xl_ref.yl_ref, ...), custom_call_target="tpu_custom_call" | custom-call | tf_op jit(solution)/shard_map/mesh/pallas_call | solution.py:470
  70.3 6.0 %all-to-all-start = ((f32[16,4,1024]{2,1,0:T(4,128)}), f32[16,4,1024]{2,1,0:T(4,128)S(1)}, u32[]{:S(2)}, u32[]{:S(2)}) async-start(f32[16,4,1024]{2,1,0:T(4,128)} %mesh.1), calls=%async_computation | async-start | bytes 524288 | tf_op jit(solution)/shard_map/all_to_all | solution.py:478
  76.9 0.3 fusion.12
  77.2 0.5 broadcast.1440
  77.7 0.7 reduce.4
  78.6 0.4 fusion.4
  79.0 3.1 %multiply_multiply_fusion.4 = f32[256,1024]{1,0:T(8,128)S(1)} fusion(f32[256,1024]{1,0:T(8,128)S(1)} %fusion.4, f32[1024]{0:T(1024)S(1)} %bitcast.129), kind=kLoop, calls=%fused_computation.74 | loop fusion | flops 19922944 | bytes 2101248 | tf_op jit(solution)/shard_map/mul | solution.py:428
  82.1 0.5 fusion.5
  82.6 0.4 fusion.7
  83.1 3.1 %multiply_multiply_fusion.2 = f32[256,1024]{1,0:T(8,128)S(1)} fusion(f32[256,1024]{1,0:T(8,128)S(1)} %fusion.7, f32[1024]{0:T(1024)S(1)} %bitcast.128), kind=kLoop, calls=%fused_computation.64 | loop fusion | flops 19922944 | bytes 2101248 | tf_op jit(solution)/shard_map/mul | solution.py:428
  86.2 0.5 fusion.8
  86.7 0.4 fusion.10
  87.2 3.1 %multiply_multiply_fusion = f32[256,1024]{1,0:T(8,128)S(1)} fusion(f32[256,1024]{1,0:T(8,128)S(1)} %fusion.10, f32[1024]{0:T(1024)S(1)} %bitcast.127), kind=kLoop, calls=%fused_computation.54 | loop fusion | flops 19922944 | bytes 2101248 | tf_op jit(solution)/shard_map/mul | solution.py:428
  90.2 0.5 fusion.11
  90.7 0.4 fusion.1
  91.2 3.1 %multiply_multiply_fusion.6 = f32[256,1024]{1,0:T(8,128)S(1)} fusion(f32[256,1024]{1,0:T(8,128)S(1)} %fusion.1, f32[1024]{0:T(1024)S(1)} %bitcast.126), kind=kLoop, calls=%fused_computation.84 | loop fusion | flops 19922944 | bytes 2101248 | tf_op jit(solution)/shard_map/mul | solution.py:428
  94.3 0.5 fusion.2
  94.9 0.6 copy.17
  95.5 0.6 reshape.887
  (43 shorter events, 0.8 us)
Async XLA Ops:
  0.6 75.7 %copy-start.3 = (s32[1,1,4,4]{3,2,1,0:T(4,128)S(1)}, s32[1,1,4,4]{3,2,1,0:T(4,128)}, u32[]{:S(2)}) copy-start(s32[1,1,4,4]{3,2,1,0:T(4,128)} %param.12) | copy-start | bytes 196
  16.7 59.7 %copy-start = (f32[16,4,1024]{2,1,0:T(4,128)S(1)}, f32[16,4,1024]{2,1,0:T(4,128)}, u32[]{:S(2)}) copy-start(f32[16,4,1024]{2,1,0:T(4,128)} %share.1.atoms_ref) | copy-start | bytes 786436
  70.3 25.2 %all-to-all-start = ((f32[16,4,1024]{2,1,0:T(4,128)}), f32[16,4,1024]{2,1,0:T(4,128)S(1)}, u32[]{:S(2)}, u32[]{:S(2)}) async-start(f32[16,4,1024]{2,1,0:T(4,128)} %mesh.1), calls=%async_computation | async-start | bytes 524288 | tf_op jit(solution)/shard_map/all_to_all | solution.py:478
  76.3 0.9 copy-start.1
  76.4 1.3 %copy-start.2 = (f32[1,1,1024]{2,1,0:T(1,128)S(1)}, f32[1,1,1024]{2,1,0:T(1,128)}, u32[]{:S(2)}) copy-start(f32[1,1,1024]{2,1,0:T(1,128)} %param.11) | copy-start | bytes 12292
